TPU v7x, 32 devices: a whole 2x2x4 slice. The times are simulated.
32 devices in a mesh: fsdp: 32 (over z, y, x, core).
Axes of the slice: x: 2, y: 2, z: 4, core: 2. Of those that a mesh axis runs over, the one named last changes fastest.
Arguments:
- tokens: bfloat16 [32768, 640], P('fsdp'), may hold values from -6 to 6
- cotangent: bfloat16 [32768, 640], P('fsdp'), may hold values from -6 to 6
- seq_lens: int32 [128], P('fsdp'), may hold values from 0 to 1024, as said below
- seq_starts: int32 [128], P('fsdp'), may hold values from 0 to 1024, as said below
- input_gain: bfloat16 [640], P('fsdp'), may hold values from 0.099609375 to 1.8984375
- w_query: bfloat16 [640, 1024], P('fsdp'), may hold values from -0.25 to 0.25
- w_key: bfloat16 [640, 256], P('fsdp'), may hold values from -0.25 to 0.25
- w_value: bfloat16 [640, 256], P('fsdp'), may hold values from -0.25 to 0.25
- query_gain: bfloat16 [256], P('fsdp'), may hold values from 0.099609375 to 1.8984375
- key_gain: bfloat16 [256], P('fsdp'), may hold values from 0.099609375 to 1.8984375
- w_output: bfloat16 [1024, 640], P('fsdp'), may hold values from -0.1875 to 0.1875
- attn_post_gain: bfloat16 [640], P('fsdp'), may hold values from 0.099609375 to 1.8984375
- ffn_pre_gain: bfloat16 [640], P('fsdp'), may hold values from 0.099609375 to 1.8984375
- w_gate: bfloat16 [640, 2048], P('fsdp'), may hold values from -0.25 to 0.25
- w_up: bfloat16 [640, 2048], P('fsdp'), may hold values from -0.25 to 0.25
- w_down: bfloat16 [2048, 640], P('fsdp'), may hold values from -0.125 to 0.125
- ffn_post_gain: bfloat16 [640], P('fsdp'), may hold values from 0.099609375 to 1.8984375
Outputs:
- result: bfloat16 [32768, 640], P('fsdp')
- grad_tokens: float32 [32768, 640], P('fsdp')
- grad_input_gain: float32 [640], P('fsdp')
- grad_w_query: float32 [640, 1024], P('fsdp')
- grad_w_key: float32 [640, 256], P('fsdp')
- grad_w_value: float32 [640, 256], P('fsdp')
- grad_query_gain: float32 [256], P('fsdp')
- grad_key_gain: float32 [256], P('fsdp')
- grad_w_output: float32 [1024, 640], P('fsdp')
- grad_attn_post_gain: float32 [640], P('fsdp')
- grad_ffn_pre_gain: float32 [640], P('fsdp')
- grad_w_gate: float32 [640, 2048], P('fsdp')
- grad_w_up: float32 [640, 2048], P('fsdp')
- grad_w_down: float32 [2048, 640], P('fsdp')
- grad_ffn_post_gain: float32 [640], P('fsdp')
Inputs may be any that keep to these rules, and one draw needn't show every extreme that they name: `seq_lens`: on each device its 4 sequence slots lie end to end from token slot 0 in the order given, so seq_starts is the sum of the lengths before it on that device; a length may be 0; every device has 256 or more slots inside sequences; some device holds one sequence of exactly 1024 tokens, filling it. `seq_starts`: the start of each sequence slot, as described for seq_lens.
All inputs are finite; a program needn't handle non-finite values.
Results may differ from a plain program's by a relative error of at most 0.017.
Values may be sent and summed in bfloat16 or wider, within the bound.
No kernel may reach another device: no remote copies, remote signals or barrier semaphores. Data moves between devices by JAX's collectives and lax.ppermute only.
A program may use at most 192 MiB of HBM per device.

v0:
```python
import functools

import jax
import jax.numpy as jnp
from jax import lax
from jax.experimental import pallas as pl
from jax.experimental.pallas import tpu as pltpu
from jax.sharding import PartitionSpec as P

AX = "fsdp"
epsilon = 1e-06
rope_base = 1000000.0
BF = jnp.bfloat16
F32 = jnp.float32
LANES = 128
TILE = 256
STEP_ROWS = 80
GELU_C = 0.7978845608028654
GELU_K = 0.044715
BIG = -1e30


def mm(a, b):
    return lax.dot_general(a, b, (((1,), (0,)), ((), ())), preferred_element_type=F32)


def mm_bt(a, b):
    return lax.dot_general(a, b, (((1,), (1,)), ((), ())), preferred_element_type=F32)


def mm_at(a, b):
    return lax.dot_general(a, b, (((0,), (0,)), ((), ())), preferred_element_type=F32)


def row_mean(v):
    return jnp.mean(v, axis=-1, keepdims=True)


def fold_rows(v):
    return jnp.sum(v.reshape(v.shape[0] // 8, 8, v.shape[1]), axis=0)


def turn(v, cos, sin):
    half = v.shape[1] // 2
    a, b = v[:, :half], v[:, half:]
    return jnp.concatenate([a * cos - b * sin, b * cos + a * sin], axis=1)


def turn_back(v, cos, sin):
    half = v.shape[1] // 2
    a, b = v[:, :half], v[:, half:]
    return jnp.concatenate([a * cos + b * sin, b * cos - a * sin], axis=1)


def norm_back(du, unit, scale):
    return scale * (du - unit * row_mean(du * unit))


def slot_starts(slot, lens_ref, starts_ref):
    first = slot
    inside = jnp.zeros(slot.shape, F32)
    for s in range(lens_ref.shape[0]):
        member = (slot >= starts_ref[s]) & (slot < starts_ref[s] + lens_ref[s])
        first = jnp.where(member, starts_ref[s], first)
        inside = jnp.where(member, 1.0, inside)
    return first, inside


class Pack:
    def __init__(self, chips, narrow, tall):
        self.chips = chips
        self.narrow = narrow
        self.tall = tall
        self.pair = narrow[0][0] // chips
        self.chips_per_step = STEP_ROWS // self.pair
        self.steps = chips // self.chips_per_step
        at = 0
        self.narrow_at = []
        for _, cols in narrow:
            self.narrow_at.append(at)
            at += cols // (2 * LANES) * self.pair
        self.tall_at = []
        for rows, cols in tall:
            self.tall_at.append(at)
            at += cols // LANES * (rows // (2 * chips))
        self.used = at

    def unpack(self, step, slabs, narrow_refs, tall_refs):
        slabs = [[value[: self.used].astype(F32) for value in pair] for pair in slabs]
        at_row = pl.multiple_of(step * STEP_ROWS, 16)
        for (_, cols), start, out in zip(self.narrow, self.narrow_at, narrow_refs):
            tiles = cols // (2 * LANES)
            for p in range(2):
                for t in range(tiles):
                    lo = start + t * self.pair
                    value = jnp.concatenate([s[p][lo : lo + self.pair] for s in slabs], axis=0)
                    col = (p * tiles + t) * LANES
                    out[pl.ds(at_row, STEP_ROWS), col : col + LANES] = value.astype(BF)
        for (rows, cols), start, out in zip(self.tall, self.tall_at, tall_refs):
            own = rows // (2 * self.chips)
            group = self.chips_per_step * 2 * own
            at_tall = pl.multiple_of(step * group, 16)
            for t in range(cols // LANES):
                lo = start + t * own
                value = jnp.concatenate(
                    [s[p][lo : lo + own] for s in slabs for p in range(2)], axis=0
                )
                out[pl.ds(at_tall, group), t * LANES : (t + 1) * LANES] = value.astype(BF)

    def pack(self, step, core, narrow_refs, tall_refs, keep_ref, send_ref):
        at_row = pl.multiple_of(step * STEP_ROWS, 8)
        pieces = [[[] for _ in range(2)] for _ in range(self.chips_per_step)]
        for (_, cols), acc in zip(self.narrow, narrow_refs):
            tiles = cols // (2 * LANES)
            for p in range(2):
                for t in range(tiles):
                    col = (p * tiles + t) * LANES
                    value = acc[pl.ds(at_row, STEP_ROWS), col : col + LANES]
                    for j in range(self.chips_per_step):
                        pieces[j][p].append(value[j * self.pair : (j + 1) * self.pair])
        for (rows, cols), acc in zip(self.tall, tall_refs):
            own = rows // (2 * self.chips)
            group = self.chips_per_step * 2 * own
            at_tall = pl.multiple_of(step * group, 8)
            for t in range(cols // LANES):
                value = acc[pl.ds(at_tall, group), t * LANES : (t + 1) * LANES]
                for j in range(self.chips_per_step):
                    for p in range(2):
                        lo = (2 * j + p) * own
                        pieces[j][p].append(value[lo : lo + own])
        for j in range(self.chips_per_step):
            first = jnp.concatenate(pieces[j][0], axis=0)
            second = jnp.concatenate(pieces[j][1], axis=0)
            keep_ref[j] = jnp.where(core == 0, first, second).astype(BF)
            send_ref[j] = jnp.where(core == 0, second, first).astype(BF)


def forward_kernel(
    pack, heads,
    lens_ref, starts_ref, place_ref, *refs,
):
    count = pack.chips_per_step
    mine_refs, other_refs, refs = refs[:count], refs[count : 2 * count], refs[2 * count :]
    (
        x_ref, cos_ref, sin_ref, gin_ref, gq_ref, gk_ref,
        w_out, h1_ref, qraw_ref, kraw_ref, qn_ref, kn_ref, v_ref, ob_ref,
        w_s, k_s, v_s, bias_s,
    ) = refs
    step = pl.program_id(0)
    hd = gk_ref.shape[1]
    model = x_ref.shape[1]
    wide = heads * hd

    @pl.when(step < pack.steps)
    def _():
        first = place_ref[0] == 0
        slabs = []
        for mine_ref, other_ref in zip(mine_refs, other_refs):
            mine, other = mine_ref[0].astype(F32), other_ref[0].astype(F32)
            slabs.append([jnp.where(first, mine, other), jnp.where(first, other, mine)])
        pack.unpack(step, slabs, [w_s.at[:, :wide], w_s.at[:, wide : wide + hd], w_s.at[:, wide + hd :]], [])
        w_out[...] = w_s[pl.ds(pl.multiple_of(step * STEP_ROWS, 16), STEP_ROWS), :]

    tile = step - pack.steps

    @pl.when(tile >= 0)
    def _():
        x = x_ref[...].astype(F32)
        scale = lax.rsqrt(row_mean(x * x) + epsilon)
        h1 = (x * scale * gin_ref[...]).astype(BF)
        h1_ref[...] = h1
        cos, sin = cos_ref[...], sin_ref[...]
        raw = mm(h1, w_s[:, :wide])
        qraw_ref[...] = raw
        for h in range(heads):
            part = raw[:, h * hd : (h + 1) * hd]
            unit = part * lax.rsqrt(row_mean(part * part) + epsilon)
            qn_ref[:, h * hd : (h + 1) * hd] = (turn(unit * gq_ref[...], cos, sin) * 0.0625).astype(BF)
        kraw = mm(h1, w_s[:, wide : wide + hd])
        kraw_ref[...] = kraw
        unit = kraw * lax.rsqrt(row_mean(kraw * kraw) + epsilon)
        kn = turn(unit * gk_ref[...], cos, sin).astype(BF)
        kn_ref[...] = kn
        v = mm(h1, w_s[:, wide + hd :]).astype(BF)
        v_ref[...] = v
        at = pl.multiple_of(tile * TILE, TILE)
        k_s[pl.ds(at, TILE), :] = kn
        v_s[pl.ds(at, TILE), :] = v

    for c in range(k_s.shape[0] // TILE):

        @pl.when(tile == c)
        def _():
            span = (c + 1) * TILE
            slot = c * TILE + lax.broadcasted_iota(jnp.int32, (TILE, 1), 0)
            first, _ = slot_starts(slot, lens_ref, starts_ref)
            other = lax.broadcasted_iota(jnp.int32, (TILE, span), 1)
            bias_s[:, :span] = jnp.where((other >= first) & (other <= slot), 0.0, BIG)
            for h in range(heads):
                q = qn_ref[:, h * hd : (h + 1) * hd]
                s = mm_bt(q, k_s[:span, :]) + bias_s[:, :span]
                e = jnp.exp(s - jnp.max(s, axis=-1, keepdims=True))
                inv = 1.0 / jnp.sum(e, axis=-1, keepdims=True)
                o = mm((e * inv).astype(BF), v_s[:span, :])
                ob_ref[:, h * hd : (h + 1) * hd] = o.astype(BF)


def middle_kernel(
    pack, tiles,
    lens_ref, starts_ref, core_ref, g_ref, x_ref, ob_ref, ct_ref, gpost_ref, gpre_ref, gffn_ref,
    res_ref, dx1_ref, dob_ref, dgains_ref, keep_ref, send_ref,
    wg_s, wu_s, wo_s, wd_s, ag_s, au_s, ao_s, ad_s, gain_s,
):
    step = pl.program_id(0)

    @pl.when(step == 0)
    def _():
        for ref in (ag_s, au_s, ao_s, ad_s, gain_s):
            ref[...] = jnp.zeros(ref.shape, F32)

    @pl.when(step < pack.steps)
    def _():
        slabs = [[g_ref[j, p] for p in range(2)] for j in range(pack.chips_per_step)]
        pack.unpack(step, slabs, [wg_s, wu_s], [wo_s, wd_s])

    tile = step - pack.steps

    @pl.when((tile >= 0) & (tile < tiles))
    def _():
        slot = tile * TILE + lax.broadcasted_iota(jnp.int32, (TILE, 1), 0)
        _, live = slot_starts(slot, lens_ref, starts_ref)
        ob = ob_ref[...]
        attn = mm(ob, wo_s[...])
        r1 = lax.rsqrt(row_mean(attn * attn) + epsilon)
        na = attn * r1
        x1 = x_ref[...].astype(F32) + na * gpost_ref[...]
        r2 = lax.rsqrt(row_mean(x1 * x1) + epsilon)
        n1 = x1 * r2
        h2 = (n1 * gpre_ref[...]).astype(BF)
        gate = mm(h2, wg_s[...])
        up = mm(h2, wu_s[...])
        th = jnp.tanh(GELU_C * (gate + GELU_K * gate * gate * gate))
        half = 0.5 * (1.0 + th)
        gl = gate * half
        slope = half + 0.5 * gate * (1.0 - th * th) * (GELU_C * (1.0 + 3.0 * GELU_K * gate * gate))
        act = (gl * up).astype(BF)
        f = mm(act, wd_s[...])
        r3 = lax.rsqrt(row_mean(f * f) + epsilon)
        nf = f * r3
        res_ref[...] = (live * (x1 + nf * gffn_ref[...])).astype(BF)
        dy = live * ct_ref[...].astype(F32)
        gain_s[0] += fold_rows(dy * nf)
        df = norm_back(dy * gffn_ref[...], nf, r3).astype(BF)
        dact = mm_bt(df, wd_s[...])
        ad_s[...] += mm_at(act, df)
        dgate = (dact * up * slope).astype(BF)
        dup = (dact * gl).astype(BF)
        ag_s[...] += mm_at(h2, dgate)
        au_s[...] += mm_at(h2, dup)
        dh2 = mm_bt(dgate, wg_s[...]) + mm_bt(dup, wu_s[...])
        gain_s[1] += fold_rows(dh2 * n1)
        dx1 = dy + norm_back(dh2 * gpre_ref[...], n1, r2)
        dx1_ref[...] = dx1
        gain_s[2] += fold_rows(dx1 * na)
        dattn = norm_back(dx1 * gpost_ref[...], na, r1).astype(BF)
        ao_s[...] += mm_at(ob, dattn)
        dob_ref[...] = mm_bt(dattn, wo_s[...]).astype(BF)

    @pl.when(tile >= tiles)
    def _():
        pack.pack(tile - tiles, core_ref[0], [ag_s, au_s], [ao_s, ad_s], keep_ref, send_ref)
        dgains_ref[...] = gain_s[...]


def backward_kernel(
    pack, heads, tiles,
    lens_ref, starts_ref, core_ref, w_ref, x_ref, dx1_ref, h1_ref, qraw_ref, kraw_ref, qn_ref, dob_ref,
    k_ref, v_ref, cos_ref, sin_ref, gin_ref, gq_ref, gk_ref,
    gt_ref, dgin_ref, dgq_ref, dgk_ref, keep_ref, send_ref,
    dq_s, dk_s, dv_s, bias_s, acc_s, dqr_s,
):
    step = pl.program_id(0)
    hd = gk_ref.shape[1]
    wide = heads * hd

    @pl.when(step == 0)
    def _():
        for ref in (dk_s, dv_s, acc_s, dgin_ref, dgq_ref, dgk_ref):
            ref[...] = jnp.zeros(ref.shape, F32)

    for c in range(tiles):

        @pl.when(step == tiles - 1 - c)
        def _():
            span = (c + 1) * TILE
            slot = c * TILE + lax.broadcasted_iota(jnp.int32, (1, TILE), 1)
            first, _ = slot_starts(slot, lens_ref, starts_ref)
            other = lax.broadcasted_iota(jnp.int32, (span, TILE), 0)
            bias_s[:span, :] = jnp.where((other >= first) & (other <= slot), 0.0, BIG)
            for h in range(heads):
                q = qn_ref[:, h * hd : (h + 1) * hd]
                dob = dob_ref[:, h * hd : (h + 1) * hd]
                s = mm_bt(k_ref[:span, :], q) + bias_s[:span, :]
                e = jnp.exp(s - jnp.max(s, axis=0, keepdims=True))
                p = e * (1.0 / jnp.sum(e, axis=0, keepdims=True))
                dv_s[:span, :] += mm(p.astype(BF), dob)
                dp = mm_bt(v_ref[:span, :], dob)
                ds = (p * (dp - jnp.sum(p * dp, axis=0, keepdims=True))).astype(BF)
                dk_s[:span, :] += mm(ds, q)
                dq_s[:, h * hd : (h + 1) * hd] = mm_at(ds, k_ref[:span, :])

    @pl.when(step < tiles)
    def _():
        at = pl.multiple_of((tiles - 1 - step) * TILE, TILE)
        cos, sin = cos_ref[...], sin_ref[...]
        for h in range(heads):
            d = turn_back(dq_s[:, h * hd : (h + 1) * hd], cos, sin) * 0.0625
            part = qraw_ref[:, h * hd : (h + 1) * hd]
            scale = lax.rsqrt(row_mean(part * part) + epsilon)
            unit = part * scale
            dgq_ref[...] += fold_rows(d * unit)
            dqr_s[:, h * hd : (h + 1) * hd] = norm_back(d * gq_ref[...], unit, scale).astype(BF)
        d = turn_back(dk_s[pl.ds(at, TILE), :], cos, sin)
        part = kraw_ref[...]
        scale = lax.rsqrt(row_mean(part * part) + epsilon)
        unit = part * scale
        dgk_ref[...] += fold_rows(d * unit)
        dqr_s[:, wide : wide + hd] = norm_back(d * gk_ref[...], unit, scale).astype(BF)
        dqr_s[:, wide + hd :] = dv_s[pl.ds(at, TILE), :].astype(BF)
        acc_s[...] += mm_at(h1_ref[...], dqr_s[...])
        dh1 = mm_bt(dqr_s[...], w_ref[...])
        x = x_ref[...].astype(F32)
        scale = lax.rsqrt(row_mean(x * x) + epsilon)
        unit = x * scale
        dgin_ref[...] += fold_rows(dh1 * unit)
        gt_ref[...] = dx1_ref[...] + norm_back(dh1 * gin_ref[...], unit, scale)

    @pl.when(step >= tiles)
    def _():
        accs = [acc_s.at[:, :wide], acc_s.at[:, wide : wide + hd], acc_s.at[:, wide + hd :]]
        pack.pack(step - tiles, core_ref[0], accs, [], keep_ref, send_ref)


def smem():
    return pl.BlockSpec(memory_space=pltpu.SMEM)


def whole(shape):
    zeros = (0,) * len(shape)
    return pl.BlockSpec(shape, lambda s: zeros)


def resident(shape):
    zeros = (0,) * len(shape)
    return pl.BlockSpec(shape, lambda s: zeros, pipeline_mode=pl.Buffered(1))


def params(megabytes):
    return pltpu.CompilerParams(
        dimension_semantics=("arbitrary",), vmem_limit_bytes=megabytes * 1024 * 1024
    )


def shape(dims, kind):
    return jax.ShapeDtypeStruct(dims, kind)


def run_forward(pack, heads, lens, starts, place, mine, other, tokens, cos, sin, gin, gq, gk):
    slots, model = tokens.shape
    hd = gk.shape[1]
    wide = heads * hd
    cols = wide + 2 * hd
    last = pack.steps - 1
    count = pack.chips_per_step

    def tile_spec(width):
        return pl.BlockSpec((TILE, width), lambda s, *_: (jnp.maximum(s - pack.steps, 0), 0))

    def fixed(width):
        return pl.BlockSpec((1, width), lambda s, *_: (0, 0))

    def slab(j):
        def index(s, lens_ref, starts_ref, place_ref):
            far = (jnp.minimum(s, last) * count + j) ^ place_ref[1]
            turned = jnp.int32(0)
            left = pack.chips
            while left > 1:
                turned = turned * 4 + far % 4
                far, left = far // 4, left // 4
            return turned, 0, 0

        return pl.BlockSpec((1, mine.shape[1], LANES), index)

    return pl.pallas_call(
        functools.partial(forward_kernel, pack, heads),
        grid_spec=pltpu.PrefetchScalarGridSpec(
            num_scalar_prefetch=3,
            grid=(pack.steps + slots // TILE,),
            in_specs=[slab(j) for j in range(count)] * 2
            + [tile_spec(model), tile_spec(hd // 2), tile_spec(hd // 2), fixed(model), fixed(hd), fixed(hd)],
            out_specs=[
                pl.BlockSpec((STEP_ROWS, cols), lambda s, *_: (jnp.minimum(s, last), 0)),
                tile_spec(model), tile_spec(wide), tile_spec(hd), tile_spec(wide), tile_spec(hd), tile_spec(hd),
                tile_spec(wide),
            ],
            scratch_shapes=[
                pltpu.VMEM((model, cols), BF), pltpu.VMEM((slots, hd), BF), pltpu.VMEM((slots, hd), BF),
                pltpu.VMEM((TILE, slots), F32),
            ],
        ),
        out_shape=[
            shape((model, cols), BF), shape((slots, model), BF), shape((slots, wide), F32),
            shape((slots, hd), F32), shape((slots, wide), BF), shape((slots, hd), BF), shape((slots, hd), BF),
            shape((slots, wide), BF),
        ],
        compiler_params=params(48),
        cost_estimate=pl.CostEstimate(
            flops=2 * slots * model * cols + 4 * slots * slots * wide // 2,
            bytes_accessed=16 * 1024 * 1024, transcendentals=heads * slots * slots,
        ),
        name="attention_forward",
    )(lens, starts, place, *([mine] * count), *([other] * count), tokens, cos, sin, gin, gq, gk)


def run_middle(pack, lens, starts, core, gathered, tokens, ob, cotangent, gpost, gpre, gffn):
    slots, model = tokens.shape
    wide = ob.shape[1]
    ff = pack.narrow[0][1]
    tiles = slots // TILE
    last = pack.steps - 1

    def tile_spec(width):
        return pl.BlockSpec((TILE, width), lambda s: (jnp.clip(s - pack.steps, 0, tiles - 1), 0))

    def out_packed():
        return pl.BlockSpec(
            (pack.chips_per_step, pack.used, LANES),
            lambda s: (jnp.maximum(s - pack.steps - tiles, 0), 0, 0),
        )

    packed = pl.BlockSpec(
        (pack.chips_per_step, 2, gathered.shape[2], LANES), lambda s: (jnp.minimum(s, last), 0, 0, 0)
    )
    return pl.pallas_call(
        functools.partial(middle_kernel, pack, tiles),
        grid=(2 * pack.steps + tiles,),
        in_specs=[
            smem(), smem(), smem(), packed, tile_spec(model), tile_spec(wide), tile_spec(model),
            whole((1, model)), whole((1, model)), whole((1, model)),
        ],
        out_specs=[
            tile_spec(model), tile_spec(model), tile_spec(wide), whole((3, 8, model)), out_packed(), out_packed(),
        ],
        out_shape=[
            shape((slots, model), BF), shape((slots, model), F32), shape((slots, wide), BF),
            shape((3, 8, model), F32),
            shape((pack.chips, pack.used, LANES), BF), shape((pack.chips, pack.used, LANES), BF),
        ],
        scratch_shapes=[
            pltpu.VMEM((model, ff), BF), pltpu.VMEM((model, ff), BF), pltpu.VMEM((wide, model), BF),
            pltpu.VMEM((ff, model), BF),
            pltpu.VMEM((model, ff), F32), pltpu.VMEM((model, ff), F32), pltpu.VMEM((wide, model), F32),
            pltpu.VMEM((ff, model), F32), pltpu.VMEM((3, 8, model), F32),
        ],
        compiler_params=params(60),
        cost_estimate=pl.CostEstimate(
            flops=6 * slots * model * (3 * ff + wide), bytes_accessed=36 * 1024 * 1024,
            transcendentals=slots * ff,
        ),
        name="output_and_ffn",
    )(lens, starts, core, gathered, tokens, ob, cotangent, gpost, gpre, gffn)


def run_backward(pack, heads, lens, starts, core, weights, tokens, dx1, h1, qraw, kraw, qn, dob, kn, v, cos, sin, gin, gq, gk):
    slots, model = tokens.shape
    hd = gk.shape[1]
    wide = heads * hd
    cols = wide + 2 * hd
    tiles = slots // TILE

    def tile_spec(width):
        return pl.BlockSpec((TILE, width), lambda s: (jnp.maximum(tiles - 1 - s, 0), 0))

    def out_packed():
        return pl.BlockSpec(
            (pack.chips_per_step, pack.used, LANES), lambda s: (jnp.maximum(s - tiles, 0), 0, 0)
        )

    return pl.pallas_call(
        functools.partial(backward_kernel, pack, heads, tiles),
        grid=(tiles + pack.steps,),
        in_specs=[
            smem(), smem(), smem(), resident((model, cols)), tile_spec(model), tile_spec(model), tile_spec(model),
            tile_spec(wide), tile_spec(hd), tile_spec(wide), tile_spec(wide), resident((slots, hd)), resident((slots, hd)),
            tile_spec(hd // 2), tile_spec(hd // 2), whole((1, model)), whole((1, hd)), whole((1, hd)),
        ],
        out_specs=[
            tile_spec(model), whole((8, model)), whole((8, hd)), whole((8, hd)), out_packed(), out_packed(),
        ],
        out_shape=[
            shape((slots, model), F32), shape((8, model), F32), shape((8, hd), F32), shape((8, hd), F32),
            shape((pack.chips, pack.used, LANES), BF), shape((pack.chips, pack.used, LANES), BF),
        ],
        scratch_shapes=[
            pltpu.VMEM((TILE, wide), F32), pltpu.VMEM((slots, hd), F32), pltpu.VMEM((slots, hd), F32),
            pltpu.VMEM((slots, TILE), F32), pltpu.VMEM((model, cols), F32), pltpu.VMEM((TILE, cols), BF),
        ],
        compiler_params=params(56),
        cost_estimate=pl.CostEstimate(
            flops=4 * slots * model * cols + 10 * slots * slots * wide // 2,
            bytes_accessed=24 * 1024 * 1024, transcendentals=heads * slots * slots,
        ),
        name="attention_backward",
    )(lens, starts, core, weights, tokens, dx1, h1, qraw, kraw, qn, dob, kn, v, cos, sin, gin, gq, gk)


def format_base4(value, digits):
    return [str((value >> (2 * d)) % 4) for d in reversed(range(digits))]


class Mover:
    def __init__(self, device_count):
        self.n = device_count
        self.chips = device_count // 2
        self.digits = 0
        while 4 ** (self.digits + 1) <= self.chips:
            self.digits += 1
        me = lax.axis_index(AX)
        self.core = me % 2
        self.chip = me // 2

    def swap(self, value, mask=1):
        return lax.ppermute(value, AX, [(i, i ^ mask) for i in range(self.n)])

    def in_core_order(self, mine, other):
        first = self.core == 0
        return jnp.where(first, mine, other), jnp.where(first, other, mine)

    def trade_halves(self, narrow):
        halves = [jnp.split(w, 2, axis=1) for w in narrow]
        low = jnp.concatenate([h[0] for h in halves], axis=1)
        high = jnp.concatenate([h[1] for h in halves], axis=1)
        first = self.core == 0
        mine = jnp.where(first, low, high)
        other = self.swap(jnp.where(first, high, low))
        return jnp.concatenate(self.in_core_order(mine, other), axis=0)

    def tiled(self, blocks):
        tiles = [b.reshape(b.shape[0], -1, LANES).transpose(1, 0, 2).reshape(-1, LANES) for b in blocks]
        return jnp.concatenate(tiles, axis=0)

    def gather_near(self, block):
        got = block[None]
        for digit in reversed(range(self.digits)):
            got = jnp.concatenate(
                [got] + [self.swap(got, j << (2 * digit + 1)) for j in (1, 2, 3)], axis=0
            )
        return got

    def by_digits(self, value):
        return value.reshape((4,) * self.digits + value.shape[1:])

    def shares(self, parts, digit, left):
        here = (self.chip >> (2 * digit)) % 4
        axis = left.index(digit)
        out = []
        for j in range(4):
            total = None
            for part in parts:
                value = lax.dynamic_index_in_dim(part, here ^ j, axis, keepdims=False).astype(F32)
                total = value if total is None else total + value
            out.append(total if j == 0 else total.astype(BF))
        return out

    def scatter(self, value, digit):
        step = 2 * 4**digit
        firsts = [i for i in range(self.n) if i // step % 4 == 0]
        groups = [[i + k * step for k in range(4)] for i in firsts]
        return lax.psum_scatter(value, AX, scatter_dimension=0, axis_index_groups=groups)

    def trade(self, shares, digit):
        return [shares[0]] + [self.swap(shares[j], j << (2 * digit + 1)) for j in (1, 2, 3)]

    def total(self, parts):
        value = parts[0].astype(F32)
        for part in parts[1:]:
            value = value + part.astype(F32)
        return value

    def split_narrow(self, total, pack):
        rows = pack.pair // 2
        count = sum(cols // (2 * LANES) for _, cols in pack.narrow)
        tiles = total[: count * pack.pair].reshape(-1, 2, rows, LANES)
        mine = lax.dynamic_index_in_dim(tiles, self.core, 1, keepdims=False)
        other = self.swap(lax.dynamic_index_in_dim(tiles, 1 - self.core, 1, keepdims=False))
        halves = self.in_core_order(mine, other)
        outs, at = [], 0
        for _, cols in pack.narrow:
            t = cols // (2 * LANES)
            both = jnp.stack([h[at : at + t] for h in halves])
            outs.append(both.transpose(2, 0, 1, 3).reshape(rows, cols))
            at += t
        return outs

    def split_tall(self, total, pack):
        outs = []
        for (rows, cols), at in zip(pack.tall, pack.tall_at):
            own, t = rows // self.n, cols // LANES
            piece = total[at : at + t * own].reshape(t, own, LANES)
            outs.append(piece.transpose(1, 0, 2).reshape(own, cols))
        return outs


def on_device(
    device_count,
    tokens,
    cotangent,
    seq_lens,
    seq_starts,
    input_gain,
    w_query,
    w_key,
    w_value,
    query_gain,
    key_gain,
    w_output,
    attn_post_gain,
    ffn_pre_gain,
    w_gate,
    w_up,
    w_down,
    ffn_post_gain,
):
    mover = Mover(device_count)
    chips = mover.chips
    slots, model = tokens.shape
    hd = w_key.shape[1]
    heads = w_query.shape[1] // hd
    ffn = Pack(
        chips,
        [(model, w_gate.shape[1]), (model, w_up.shape[1])],
        [(w_output.shape[0] * device_count, model), (w_down.shape[0] * device_count, model)],
    )
    attn = Pack(chips, [(model, heads * hd), (model, hd), (model, hd)], [])

    gains = [input_gain, query_gain, key_gain, attn_post_gain, ffn_pre_gain, ffn_post_gain]
    flat = jnp.concatenate(gains)
    flat = jnp.pad(flat, (0, 8 * LANES - flat.shape[0])).reshape(8, LANES)
    narrow = mover.trade_halves([w_gate, w_up, w_query, w_key, w_value])
    split = w_gate.shape[1]
    far = lax.all_gather(mover.tiled([narrow[:, :split], w_output, w_down]), AX, axis=0)
    gathered = far.reshape(chips, 2, ffn.used, LANES)
    mine = mover.gather_near(mover.tiled([narrow[:, split:], flat]))
    other = mover.swap(mine)
    both = jnp.stack(mover.in_core_order(mine[:, attn.used], other[:, attn.used]), axis=1)
    order = [int("".join(reversed(format_base4(k, mover.digits))), 4) for k in range(chips)]
    wanted = jnp.arange(chips, dtype=jnp.int32)[:, None] == (jnp.array(order, jnp.int32) ^ mover.chip)[None]
    flat = mm(wanted.astype(BF), both.reshape(chips, 2 * LANES)).reshape(device_count, LANES)
    vectors, at = [], 0
    for g in gains:
        vectors.append(flat[:, at : at + g.shape[0]].reshape(1, -1))
        at += g.shape[0]
    gin, gq, gk, gpost, gpre, gffn = vectors

    slot = jnp.arange(slots, dtype=jnp.int32)
    inside = (slot[None, :] >= seq_starts[:, None]) & (
        slot[None, :] < seq_starts[:, None] + seq_lens[:, None]
    )
    offset = jnp.sum(jnp.where(inside, seq_starts[:, None], 0), axis=0)
    frequency = rope_base ** (-2.0 * jnp.arange(hd // 2, dtype=F32) / hd)
    angles = (slot - offset).astype(F32)[:, None] * frequency[None, :]
    cos, sin = jnp.cos(angles), jnp.sin(angles)
    core = mover.core.astype(jnp.int32).reshape(1)

    place = jnp.stack([mover.core, mover.chip]).astype(jnp.int32)
    weights, h1, qraw, kraw, qn, kn, v, ob = run_forward(
        attn, heads, seq_lens, seq_starts, place, mine, other, tokens, cos, sin, gin, gq, gk
    )
    result, dx1, dob, dgains, keep, send = run_middle(
        ffn, seq_lens, seq_starts, core, gathered, tokens, ob, cotangent, gpost, gpre, gffn
    )
    up, down = list(range(mover.digits)), list(reversed(range(mover.digits)))
    cut = 3 * ffn.used // 32 * 8
    both = [mover.by_digits(keep), mover.by_digits(mover.swap(send))]
    near = mover.shares([v[..., :cut, :] for v in both], up[0], down)
    far = mover.total([v[..., cut:, :] for v in both]).astype(BF)
    dob, near, far = lax.optimization_barrier((dob, near, far))
    near = mover.trade(near, up[0])
    far = mover.scatter(far, down[0])
    grad_tokens, dgin, dgq, dgk, keep, send = run_backward(
        attn, heads, seq_lens, seq_starts, core, weights, tokens, dx1, h1, qraw, kraw, qn, dob, kn, v,
        cos, sin, gin, gq, gk,
    )
    dffn, dpre, dpost = (jnp.sum(dgains[i], axis=0) for i in range(3))
    grads = [jnp.sum(dgin, axis=0), jnp.sum(dgq, axis=0), jnp.sum(dgk, axis=0), dpost, dpre, dffn]
    flat = jnp.concatenate([g.reshape(device_count, -1) for g in grads], axis=1).astype(BF)
    flat = jnp.pad(flat, ((0, 0), (0, 8 * LANES - flat.shape[1]))).reshape(chips, 2, 8, LANES)
    keep = jnp.concatenate(
        [keep, lax.dynamic_index_in_dim(flat, mover.core, 1, keepdims=False)], axis=1
    )
    send = jnp.concatenate(
        [send, lax.dynamic_index_in_dim(flat, 1 - mover.core, 1, keepdims=False)], axis=1
    )
    send, near, far = lax.optimization_barrier((send, near, far))
    attn_parts = [mover.by_digits(keep), mover.by_digits(mover.swap(send))]
    for d in down[1:]:
        far = mover.scatter(far, d)
    for d in up:
        share = mover.shares(attn_parts, d, [k for k in down if k >= d])
        if d + 1 < mover.digits:
            near = mover.shares(near, d + 1, [k for k in down if k > d])
            share, near = lax.optimization_barrier((share, near))
            near = mover.trade(near, d + 1)
        attn_parts = mover.trade(share, d)
    far, attn_parts = lax.optimization_barrier((far, attn_parts))
    ffn_sum = jnp.concatenate([mover.total(near), far.astype(F32)], axis=0)
    attn_sum = mover.total(attn_parts)
    own_gate, own_up = mover.split_narrow(ffn_sum, ffn)
    own_output, own_down = mover.split_tall(ffn_sum, ffn)
    own_query, own_key, own_value = mover.split_narrow(attn_sum, attn)
    flat = attn_sum[attn.used :].reshape(-1)
    owned, at = [], 0
    for g in gains:
        owned.append(flat[at : at + g.shape[0]])
        at += g.shape[0]
    own_gin, own_gq, own_gk, own_gpost, own_gpre, own_gffn = owned
    return (
        result, grad_tokens, own_gin, own_query, own_key, own_value, own_gq, own_gk, own_output, own_gpost,
        own_gpre, own_gate, own_up, own_down, own_gffn,
    )


def solution(mesh):
    rows, flat = P(AX, None), P(AX)
    device_count = mesh.shape[AX]

    def block(*arrays):
        return on_device(device_count, *arrays)

    return jax.shard_map(
        block,
        mesh=mesh,
        in_specs=(
            rows, rows, flat, flat, flat, rows, rows, rows, flat, flat, rows, flat, flat, rows, rows, rows, flat,
        ),
        out_specs=(
            rows, rows, flat, rows, rows, rows, flat, flat, rows, flat, flat, rows, rows, rows, flat,
        ),
        check_vma=False,
    )
```

profile of v0, /device:TPU:9, one launch (start us, length us, event | category | flops | bytes accessed | tf_op | source)
XLA Modules:
  0.0 276.6 jit_solution(17062052571121511894)
XLA Ops:
  7.2 0.8 slice_dynamic-update-slice_fusion.3
  8.1 0.8 slice_dynamic-update-slice_fusion.2
  9.0 0.8 constant_dynamic-update-slice_fusion.2
  9.8 0.7 constant_dynamic-update-slice_fusion.1
  10.5 0.7 constant_dynamic-update-slice_fusion
  11.2 0.7 collective-permute-start
  12.0 1.0 reshape.265
  13.0 0.8 reshape.263
  14.1 0.7 pad_maximum_fusion.1
  15.3 2.5 collective-permute-start.2
  18.0 1.0 collective-permute-done.1
  19.0 2.4 collective-permute-done.2
  21.3 3.0 %collective-permute-done.3 = bf16[1,248,128]{2,1,0:T(8,128)(2,1)S(1)} collective-permute-done((bf16[1,248,128]{2,1,0:T(8,128)(2,1)S(1)}, bf16[1,248,128]{2,1,0:T(8,128)(2,1)S(1)}, u32[]{:S(2)}, u32[]{:S(2)}) %collective-permute-start.3) | collective-permute-done | bytes 63520 | tf_op jit(solution)/shard_map/ppermute | solution.py:533
  24.4 1.3 collective-permute-start.4
  25.6 1.2 collective-permute-start.5
  27.1 7.2 %collective-permute-done.4 = bf16[4,248,128]{2,1,0:T(8,128)(2,1)S(1)} collective-permute-done((bf16[4,248,128]{2,1,0:T(8,128)(2,1)S(1)}, bf16[4,248,128]{2,1,0:T(8,128)(2,1)S(1)}, u32[]{:S(2)}, u32[]{:S(2)}) %collective-permute-start.4) | collective-permute-done | bytes 253984 | tf_op jit(solution)/shard_map/ppermute | solution.py:533
  34.4 6.2 %collective-permute-done.6 = bf16[4,248,128]{2,1,0:T(8,128)(2,1)S(1)} collective-permute-done((bf16[4,248,128]{2,1,0:T(8,128)(2,1)S(1)}, bf16[4,248,128]{2,1,0:T(8,128)(2,1)S(1)}, u32[]{:S(2)}, u32[]{:S(2)}) %collective-permute-start.6) | collective-permute-done | bytes 253984 | tf_op jit(solution)/shard_map/ppermute | solution.py:533
  40.6 0.8 collective-permute-start.7
  41.7 1.9 multiply_sine_fusion
  44.4 0.7 reshape.275.gpost_ref
  45.0 0.7 reshape.276.gpre_ref
  45.7 0.7 reshape.277.gffn_ref
  46.4 16.9 %attention_forward.1 = (bf16[640,1536]{1,0:T(8,128)(2,1)}, bf16[1024,640]{1,0:T(8,128)(2,1)}, f32[1024,1024]{1,0:T(8,128)}, f32[1024,256]{1,0:T(8,128)S(1)}, bf1...) custom-call(s32[4]{0:T(128)S(1)} %copy-done.6, ...), custom_call_target="tpu_custom_call" | custom-call | flops 4160749568 | bytes 16777216 | tf_op jit(solution)/shard_map/attention_forward/pallas_call | solution.py:394
  63.4 1.0 copy-done.7
  64.4 0.8 copy-done.8
  65.2 0.8 copy-done.9
  66.0 32.3 %all-gather.3.cloned.1.call-done = bf16[35840,128]{1,0:T(8,128)(2,1)} async-done(((bf16[1120,128]{1,0:T(8,128)(2,1)}), bf16[35840,128]{1,0:T(8,128)(2,1)}) %all-gather.3.cloned.1.call-update) | async-done | bytes 9175056 | tf_op jit(solution)/shard_map/all_gather | solution.py:651
  98.3 59.6 %output_and_ffn.1 = (bf16[1024,640]{1,0:T(8,128)(2,1)}, f32[1024,640]{1,0:T(8,128)}, bf16[1024,1024]{1,0:T(8,128)(2,1)}, f32[3,8,640]{2,1,0:T(8,128)}, bf16[16,1...) custom-call(s32[4]{0:T(128)} %lens_ref.5, s32[4]{0:T(128)} %starts_ref.5, s32[1]{0:T(128)} %bitcast.core_ref, ...), custom_call_target="tpu_custom_call" | custom-call | flops 28185722880 | bytes 37748736 | tf_op jit(solution)/shard_map/output_and_ffn/pallas_call | solution.py:444
  158.3 2.2 slice.162
  160.5 5.6 %collective-permute-done.8 = bf16[16,1120,128]{2,1,0:T(8,128)(2,1)} collective-permute-done((bf16[16,1120,128]{2,1,0:T(8,128)(2,1)}, bf16[16,1120,128]{2,1,0:T(8,128)(2,1)}, u32[]{:S(2)}, u32[]{:S(2)}) %collective-permute-start.8) | collective-permute-done | bytes 4587552 | tf_op jit(solution)/shard_map/ppermute | solution.py:533
  166.1 2.9 %add_convert_fusion = bf16[4,4,280,128]{3,2,1,0:T(8,128)(2,1)} fusion(bf16[4,4,1120,128]{3,2,1,0:T(8,128)(2,1)} %bitcast.14, bf16[4,4,1120,128]{3,2,1,0:T(8,128)(2,1)} %bitcast.194), kind=kLoop, calls=%fused_computation | loop fusion | flops 2293760 | bytes 3440640 | tf_op jit(solution)/shard_map/convert_element_type | solution.py:686
  169.0 2.2 slice.163
  171.2 2.8 %fusion.2 = (bf16[4,840,128]{2,1,0:T(8,128)(2,1)}, bf16[4,840,128]{2,1,0:T(8,128)(2,1)}, bf16[4,840,128]{2,1,0:T(8,128)(2,1)}, f32[4,840,128]{2,1,0:T(8,128)}) fusion(bf16[4,4,840,128]{3,2,1,0:T(8,128)(2,1)S(1)} %slice.163, s32[]{:T(128)S(6)} %select_n.183, bf16[4,4,840,128]{3,2,1,0:T(8,128)(2,1)S(1)} %slice.162, s32[]{:T(128)S(6)} %select_n.182, ...), kind=kLoop, calls=%fused_computation.12 | loop fusion | flops 6451200 | bytes 11182096 | tf_op jit(solution)/shard_map/convert_element_type | solution.py:572
  174.5 1.1 collective-permute-start.10
  175.6 1.2 collective-permute-start.11
  177.2 42.3 %attention_backward.1 = (f32[1024,640]{1,0:T(8,128)}, f32[8,640]{1,0:T(8,128)}, f32[8,256]{1,0:T(8,128)}, f32[8,256]{1,0:T(8,128)}, bf16[16,240,128]{2,1,0:T(8,128)(2,1)}, /*index=5*/bf16[16,240,128]{2,1,0:T(8,128)(2,1)}) custom-call(s32[4]{0:T(128)} %lens_ref.5, s32[4]{0:T(128)} %starts_ref.5, s32[1]{0:T(128)} %bitcast.core_ref, ...), custom_call_target="tpu_custom_call" | custom-call | flops 9395240960 | bytes 25165824 | tf_op jit(solution)/shard_map/attention_backward/pallas_call | solution.py:489
  219.5 0.9 reduce_sum.64
  220.5 0.7 reduce_sum.65
  221.3 0.7 reduce_sum.66
  222.3 2.2 pad_maximum_fusion
  224.6 0.9 copy-done.12
  225.8 1.1 collective-permute-start.12
  227.0 3.0 %fusion.16 = (bf16[840,128]{1,0:T(8,128)(2,1)}, bf16[840,128]{1,0:T(8,128)(2,1)}, bf16[840,128]{1,0:T(8,128)(2,1)}, f32[840,128]{1,0:T(8,128)S(1)}) fusion(f32[4,840,128]{2,1,0:T(8,128)S(1)} %copy-done.10, s32[]{:T(128)S(6)} %select_n.190, bf16[4,840,128]{2,1,0:T(8,128)(2,1)} %copy-done.13, bf16[4,840,128]{2,1,0:T(8,128)(2,1)} %copy-done.12, ...), kind=kLoop, calls=%fused_computation.45 | loop fusion | flops 2903040 | bytes 5376016 | tf_op jit(solution)/shard_map/add | solution.py:571
  230.0 1.1 fusion.5
  231.3 1.6 collective-permute-start.21
  232.9 0.8 collective-permute-start.22
  233.8 1.1 collective-permute-start.13
  235.3 4.9 %collective-permute-done.20 = bf16[840,128]{1,0:T(8,128)(2,1)S(1)} collective-permute-done((bf16[840,128]{1,0:T(8,128)(2,1)}, bf16[840,128]{1,0:T(8,128)(2,1)S(1)}, u32[]{:S(2)}, u32[]{:S(2)}) %collective-permute-start.20) | collective-permute-done | bytes 215072 | tf_op jit(solution)/shard_map/ppermute | solution.py:533
  240.2 1.2 collective-permute-start.15
  241.4 1.8 collective-permute-done.21
  243.2 9.7 %collective-permute-done.22 = bf16[840,128]{1,0:T(8,128)(2,1)S(1)} collective-permute-done((bf16[840,128]{1,0:T(8,128)(2,1)}, bf16[840,128]{1,0:T(8,128)(2,1)S(1)}, u32[]{:S(2)}, u32[]{:S(2)}) %collective-permute-start.22) | collective-permute-done | bytes 215072 | tf_op jit(solution)/shard_map/ppermute | solution.py:533
  253.4 1.8 collective-permute-start.17
  255.2 0.8 collective-permute-start.18
  256.1 2.0 collective-permute-start.23
  258.2 0.7 copy.227
  259.0 2.3 collective-permute-done.18
  262.5 0.9 convert_element_type.307
  263.5 1.8 collective-permute-start.19
  265.3 0.7 copy.225
  266.3 0.6 copy.208
  266.9 0.6 copy.207
  267.6 0.7 reshape.290
  268.4 0.7 copy.211
  269.1 0.7 copy.210
  (150 shorter events, 7.2 us)
Async XLA Ops:
  7.2 91.1 %all-gather.3.cloned.1.call-start = ((), (), s32[]{:S(2)}) async-start(), calls=%async_computation.3 | async-start | bytes 9461760 | tf_op jit(solution)/shard_map/all_gather | solution.py:651
  8.9 6.0 %copy-start.5 = (s32[4]{0:T(128)S(1)}, s32[4]{0:T(128)}, u32[]{:S(2)}) copy-start(s32[4]{0:T(128)} %starts_ref.5) | copy-start | bytes 52
  8.9 6.0 %copy-start.6 = (s32[4]{0:T(128)S(1)}, s32[4]{0:T(128)}, u32[]{:S(2)}) copy-start(s32[4]{0:T(128)} %lens_ref.5) | copy-start | bytes 52
  8.9 6.0 %copy-start.15 = (bf16[20]{0:T(256)(128)(2,1)S(1)}, bf16[20]{0:T(256)(128)(2,1)}, u32[]{:S(2)}) copy-start(bf16[20]{0:T(256)(128)(2,1)} %param.22) | copy-start | bytes 124
  8.9 6.0 %copy-start.16 = (bf16[8]{0:T(256)(128)(2,1)S(1)}, bf16[8]{0:T(256)(128)(2,1)}, u32[]{:S(2)}) copy-start(bf16[8]{0:T(256)(128)(2,1)} %param.26) | copy-start | bytes 52
  8.9 6.0 %copy-start.17 = (bf16[8]{0:T(256)(128)(2,1)S(1)}, bf16[8]{0:T(256)(128)(2,1)}, u32[]{:S(2)}) copy-start(bf16[8]{0:T(256)(128)(2,1)} %param.27) | copy-start | bytes 52
  9.0 6.0 %copy-start.18 = (bf16[20]{0:T(256)(128)(2,1)S(1)}, bf16[20]{0:T(256)(128)(2,1)}, u32[]{:S(2)}) copy-start(bf16[20]{0:T(256)(128)(2,1)} %param.29) | copy-start | bytes 124
  9.0 6.0 %copy-start.19 = (bf16[20]{0:T(256)(128)(2,1)S(1)}, bf16[20]{0:T(256)(128)(2,1)}, u32[]{:S(2)}) copy-start(bf16[20]{0:T(256)(128)(2,1)} %param.30) | copy-start | bytes 124
  9.0 6.0 %copy-start.20 = (bf16[20]{0:T(256)(128)(2,1)S(1)}, bf16[20]{0:T(256)(128)(2,1)}, u32[]{:S(2)}) copy-start(bf16[20]{0:T(256)(128)(2,1)} %param.34) | copy-start | bytes 124
  11.2 2.6 collective-permute-start
  14.0 27.6 %copy-start.21 = (s32[16]{0:T(128)S(1)}, s32[16]{0:T(128)}, u32[]{:S(2)}) copy-start(s32[16]{0:T(128)} %constant.189.clone) | copy-start | bytes 196
  14.8 209.8 %reduce-scatter.5.cloned.1.call-start = ((), (), s32[]{:S(2)}) async-start(), calls=%async_computation.2 | async-start | bytes 1433600 | tf_op jit(solution)/shard_map/reduce_scatter | solution.py:579
  15.2 3.7 %collective-permute-start.1 = (bf16[1,248,128]{2,1,0:T(8,128)(2,1)S(1)}, bf16[1,248,128]{2,1,0:T(8,128)(2,1)S(1)}, u32[]{:S(2)}, u32[]{:S(2)}) collective-permute-start(bf16[1,248,128]{2,1,0:T(8,128)(2,1)S(1)} %maximum_bitcast_fusion.3), channel_id=1, source_target_pairs={{0,8},{1,9},{2,10},{3,11},{4,12},{5,13},{6,14},{7,15},{8,0},{9,1},... | collective-permute-start | bytes 190472 | tf_op jit(solution)/shard_map/ppermute | solution.py:533
  15.3 6.0 %collective-permute-start.2 = (bf16[1,248,128]{2,1,0:T(8,128)(2,1)S(1)}, bf16[1,248,128]{2,1,0:T(8,128)(2,1)S(1)}, u32[]{:S(2)}, u32[]{:S(2)}) collective-permute-start(bf16[1,248,128]{2,1,0:T(8,128)(2,1)S(1)} %maximum_bitcast_fusion.3), channel_id=1, source_target_pairs={{0,16},{1,17},{2,18},{3,19},{4,20},{5,21},{6,22},{7,23},{8,24},{9,... | collective-permute-start | bytes 190472 | tf_op jit(solution)/shard_map/ppermute | solution.py:533
  17.8 6.5 %collective-permute-start.3 = (bf16[1,248,128]{2,1,0:T(8,128)(2,1)S(1)}, bf16[1,248,128]{2,1,0:T(8,128)(2,1)S(1)}, u32[]{:S(2)}, u32[]{:S(2)}) collective-permute-start(bf16[1,248,128]{2,1,0:T(8,128)(2,1)S(1)} %maximum_bitcast_fusion.3), channel_id=1, source_target_pairs={{0,24},{1,25},{2,26},{3,27},{4,28},{5,29},{6,30},{7,31},{8,16},{9,... | collective-permute-start | bytes 190472 | tf_op jit(solution)/shard_map/ppermute | solution.py:533
  24.4 9.9 %collective-permute-start.4 = (bf16[4,248,128]{2,1,0:T(8,128)(2,1)S(1)}, bf16[4,248,128]{2,1,0:T(8,128)(2,1)S(1)}, u32[]{:S(2)}, u32[]{:S(2)}) collective-permute-start(bf16[4,248,128]{2,1,0:T(8,128)(2,1)S(1)} %pad_maximum_fusion.2), channel_id=1, source_target_pairs={{0,2},{1,3},{2,0},{3,1},{4,6},{5,7},{6,4},{7,5},{8,10},{9,11},{10,... | collective-permute-start | bytes 761864 | tf_op jit(solution)/shard_map/ppermute | solution.py:533
  25.6 8.7 %collective-permute-start.5 = (bf16[4,248,128]{2,1,0:T(8,128)(2,1)S(1)}, bf16[4,248,128]{2,1,0:T(8,128)(2,1)S(1)}, u32[]{:S(2)}, u32[]{:S(2)}) collective-permute-start(bf16[4,248,128]{2,1,0:T(8,128)(2,1)S(1)} %pad_maximum_fusion.2), channel_id=1, source_target_pairs={{0,4},{1,5},{2,6},{3,7},{4,0},{5,1},{6,2},{7,3},{8,12},{9,13},{10,... | collective-permute-start | bytes 761864 | tf_op jit(solution)/shard_map/ppermute | solution.py:533
  26.9 13.7 %collective-permute-start.6 = (bf16[4,248,128]{2,1,0:T(8,128)(2,1)S(1)}, bf16[4,248,128]{2,1,0:T(8,128)(2,1)S(1)}, u32[]{:S(2)}, u32[]{:S(2)}) collective-permute-start(bf16[4,248,128]{2,1,0:T(8,128)(2,1)S(1)} %pad_maximum_fusion.2), channel_id=1, source_target_pairs={{0,6},{1,7},{2,4},{3,5},{4,2},{5,3},{6,0},{7,1},{8,14},{9,15},{10,... | collective-permute-start | bytes 761864 | tf_op jit(solution)/shard_map/ppermute | solution.py:533
  40.6 3.0 %collective-permute-start.7 = (bf16[16,248,128]{2,1,0:T(8,128)(2,1)S(1)}, bf16[16,248,128]{2,1,0:T(8,128)(2,1)S(1)}, u32[]{:S(2)}, u32[]{:S(2)}) collective-permute-start(bf16[16,248,128]{2,1,0:T(8,128)(2,1)S(1)} %constant_dynamic-update-slice_fusion.6.refs_0_.refs_1_), channel_id=1, source_target_pairs={{0,1},{1,0},{2,3},{3,2},{4,5},{5,4},{6,7},{7,6},{8,9},{9,8},{10,11... | collective-permute-start | bytes 3047432 | tf_op jit(solution)/shard_map/ppermute | solution.py:533
  43.5 19.8 %copy-start = (f32[1024,128]{1,0:T(8,128)}, f32[1024,128]{1,0:T(8,128)S(1)}, u32[]{:S(2)}) copy-start(f32[1024,128]{1,0:T(8,128)S(1)} %get-tuple-element.160.refs_6_.sin_ref) | copy-start | bytes 1572868
  43.6 19.8 %copy-start.1 = (f32[1024,128]{1,0:T(8,128)}, f32[1024,128]{1,0:T(8,128)S(1)}, u32[]{:S(2)}) copy-start(f32[1024,128]{1,0:T(8,128)S(1)} %get-tuple-element.161.refs_5_.cos_ref) | copy-start | bytes 1572868
  44.1 19.3 %copy-start.2 = (f32[1,640]{1,0:T(1,128)}, f32[1,640]{1,0:T(1,128)S(1)}, u32[]{:S(2)}) copy-start(f32[1,640]{1,0:T(1,128)S(1)} %reshape.272.refs_7_.gin_ref) | copy-start | bytes 7684
  44.2 19.1 %copy-start.3 = (f32[1,256]{1,0:T(1,128)}, f32[1,256]{1,0:T(1,128)S(1)}, u32[]{:S(2)}) copy-start(f32[1,256]{1,0:T(1,128)S(1)} %reshape.273.refs_8_.gq_ref) | copy-start | bytes 3076
  44.3 19.0 %copy-start.4 = (f32[1,256]{1,0:T(1,128)}, f32[1,256]{1,0:T(1,128)S(1)}, u32[]{:S(2)}) copy-start(f32[1,256]{1,0:T(1,128)S(1)} %reshape.274.refs_9_.gk_ref) | copy-start | bytes 3076
  63.4 1.0 copy-start.7
  64.4 0.8 copy-start.8
  65.2 0.8 copy-start.9
  157.9 8.1 %collective-permute-start.8 = (bf16[16,1120,128]{2,1,0:T(8,128)(2,1)}, bf16[16,1120,128]{2,1,0:T(8,128)(2,1)}, u32[]{:S(2)}, u32[]{:S(2)}) collective-permute-start(bf16[16,1120,128]{2,1,0:T(8,128)(2,1)} %get-tuple-element.70), channel_id=1, source_target_pairs={{0,1},{1,0},{2,3},{3,2},{4,5},{5,4},{6,7},{7,6},{8,9},{9,8},{10,11... | collective-permute-start | bytes 13762568 | tf_op jit(solution)/shard_map/ppermute | solution.py:533
  171.2 2.9 %copy-start.14 = (f32[3,8,640]{2,1,0:T(8,128)S(1)}, f32[3,8,640]{2,1,0:T(8,128)}, u32[]{:S(2)}) copy-start(f32[3,8,640]{2,1,0:T(8,128)} %get-tuple-element.79) | copy-start | bytes 184324
  174.0 85.0 %reduce-scatter.7.cloned.1.call-start = ((), (), s32[]{:S(2)}) async-start(), calls=%async_computation.4 | async-start | bytes 358400
  174.5 50.1 %collective-permute-start.10 = (bf16[4,840,128]{2,1,0:T(8,128)(2,1)}, bf16[4,840,128]{2,1,0:T(8,128)(2,1)S(1)}, u32[]{:S(2)}, u32[]{:S(2)}) collective-permute-start(bf16[4,840,128]{2,1,0:T(8,128)(2,1)} %get-tuple-element.82), channel_id=1, source_target_pairs={{0,4},{1,5},{2,6},{3,7},{4,0},{5,1},{6,2},{7,3},{8,12},{9,13},{10,... | collective-permute-start | bytes 2580488 | tf_op jit(solution)/shard_map/ppermute | solution.py:533
  175.6 48.9 %collective-permute-start.11 = (bf16[4,840,128]{2,1,0:T(8,128)(2,1)}, bf16[4,840,128]{2,1,0:T(8,128)(2,1)S(1)}, u32[]{:S(2)}, u32[]{:S(2)}) collective-permute-start(bf16[4,840,128]{2,1,0:T(8,128)(2,1)} %get-tuple-element.83), channel_id=1, source_target_pairs={{0,6},{1,7},{2,4},{3,5},{4,2},{5,3},{6,0},{7,1},{8,14},{9,15},{10,... | collective-permute-start | bytes 2580488 | tf_op jit(solution)/shard_map/ppermute | solution.py:533
  176.8 47.8 %collective-permute-start.9 = (bf16[4,840,128]{2,1,0:T(8,128)(2,1)}, bf16[4,840,128]{2,1,0:T(8,128)(2,1)}, u32[]{:S(2)}, u32[]{:S(2)}) collective-permute-start(bf16[4,840,128]{2,1,0:T(8,128)(2,1)} %get-tuple-element.81), channel_id=1, source_target_pairs={{0,2},{1,3},{2,0},{3,1},{4,6},{5,7},{6,4},{7,5},{8,10},{9,11},{10,... | collective-permute-start | bytes 2580488 | tf_op jit(solution)/shard_map/ppermute | solution.py:533
  219.5 7.4 %copy-start.10 = (f32[4,840,128]{2,1,0:T(8,128)S(1)}, f32[4,840,128]{2,1,0:T(8,128)}, u32[]{:S(2)}) copy-start(f32[4,840,128]{2,1,0:T(8,128)} %get-tuple-element.88) | copy-start | bytes 5160964
  224.6 0.9 copy-start.12
  224.6 1.3 copy-start.13
  225.8 4.2 %collective-permute-start.12 = (bf16[16,248,128]{2,1,0:T(8,128)(2,1)}, bf16[16,248,128]{2,1,0:T(8,128)(2,1)S(1)}, u32[]{:S(2)}, u32[]{:S(2)}) collective-permute-start(bf16[16,248,128]{2,1,0:T(8,128)(2,1)} %pad_maximum_fusion), channel_id=1, source_target_pairs={{0,1},{1,0},{2,3},{3,2},{4,5},{5,4},{6,7},{7,6},{8,9},{9,8},{10,11... | collective-permute-start | bytes 3047432 | tf_op jit(solution)/shard_map/ppermute | solution.py:533
  227.0 3.1 %copy-start.11 = (bf16[16,240,128]{2,1,0:T(8,128)(2,1)S(1)}, bf16[16,240,128]{2,1,0:T(8,128)(2,1)}, u32[]{:S(2)}) copy-start(bf16[16,240,128]{2,1,0:T(8,128)(2,1)} %get-tuple-element.86) | copy-start | bytes 2949124
  231.1 9.1 %collective-permute-start.20 = (bf16[840,128]{1,0:T(8,128)(2,1)}, bf16[840,128]{1,0:T(8,128)(2,1)S(1)}, u32[]{:S(2)}, u32[]{:S(2)}) collective-permute-start(bf16[840,128]{1,0:T(8,128)(2,1)} %get-tuple-element.101), channel_id=1, source_target_pairs={{0,8},{1,9},{2,10},{3,11},{4,12},{5,13},{6,14},{7,15},{8,0},{9,1},... | collective-permute-start | bytes 645128 | tf_op jit(solution)/shard_map/ppermute | solution.py:533
  231.3 11.9 %collective-permute-start.21 = (bf16[840,128]{1,0:T(8,128)(2,1)}, bf16[840,128]{1,0:T(8,128)(2,1)S(1)}, u32[]{:S(2)}, u32[]{:S(2)}) collective-permute-start(bf16[840,128]{1,0:T(8,128)(2,1)} %get-tuple-element.102), channel_id=1, source_target_pairs={{0,16},{1,17},{2,18},{3,19},{4,20},{5,21},{6,22},{7,23},{8,24},{9,... | collective-permute-start | bytes 645128 | tf_op jit(solution)/shard_map/ppermute | solution.py:533
  232.9 20.0 %collective-permute-start.22 = (bf16[840,128]{1,0:T(8,128)(2,1)}, bf16[840,128]{1,0:T(8,128)(2,1)S(1)}, u32[]{:S(2)}, u32[]{:S(2)}) collective-permute-start(bf16[840,128]{1,0:T(8,128)(2,1)} %get-tuple-element.103), channel_id=1, source_target_pairs={{0,24},{1,25},{2,26},{3,27},{4,28},{5,29},{6,30},{7,31},{8,16},{9,... | collective-permute-start | bytes 645128 | tf_op jit(solution)/shard_map/ppermute | solution.py:533
  233.8 19.4 %collective-permute-start.13 = (bf16[4,248,128]{2,1,0:T(8,128)(2,1)}, bf16[4,248,128]{2,1,0:T(8,128)(2,1)S(1)}, u32[]{:S(2)}, u32[]{:S(2)}) collective-permute-start(bf16[4,248,128]{2,1,0:T(8,128)(2,1)} %get-tuple-element.93), channel_id=1, source_target_pairs={{0,2},{1,3},{2,0},{3,1},{4,6},{5,7},{6,4},{7,5},{8,10},{9,11},{10,... | collective-permute-start | bytes 761864 | tf_op jit(solution)/shard_map/ppermute | solution.py:533
  234.9 18.3 %collective-permute-start.14 = (bf16[4,248,128]{2,1,0:T(8,128)(2,1)}, bf16[4,248,128]{2,1,0:T(8,128)(2,1)S(1)}, u32[]{:S(2)}, u32[]{:S(2)}) collective-permute-start(bf16[4,248,128]{2,1,0:T(8,128)(2,1)} %get-tuple-element.94), channel_id=1, source_target_pairs={{0,4},{1,5},{2,6},{3,7},{4,0},{5,1},{6,2},{7,3},{8,12},{9,13},{10,... | collective-permute-start | bytes 761864 | tf_op jit(solution)/shard_map/ppermute | solution.py:533
  240.2 13.0 %collective-permute-start.15 = (bf16[4,248,128]{2,1,0:T(8,128)(2,1)S(1)}, bf16[4,248,128]{2,1,0:T(8,128)(2,1)S(1)}, u32[]{:S(2)}, u32[]{:S(2)}) collective-permute-start(bf16[4,248,128]{2,1,0:T(8,128)(2,1)S(1)} %get-tuple-element.95), channel_id=1, source_target_pairs={{0,6},{1,7},{2,4},{3,5},{4,2},{5,3},{6,0},{7,1},{8,14},{9,15},{10,... | collective-permute-start | bytes 761864 | tf_op jit(solution)/shard_map/ppermute | solution.py:533
  253.3 5.7 %collective-permute-start.16 = (bf16[248,128]{1,0:T(8,128)(2,1)S(1)}, bf16[248,128]{1,0:T(8,128)(2,1)S(1)}, u32[]{:S(2)}, u32[]{:S(2)}) collective-permute-start(bf16[248,128]{1,0:T(8,128)(2,1)S(1)} %get-tuple-element.124), channel_id=1, source_target_pairs={{0,8},{1,9},{2,10},{3,11},{4,12},{5,13},{6,14},{7,15},{8,0},{9,1},... | collective-permute-start | bytes 190472 | tf_op jit(solution)/shard_map/ppermute | solution.py:533
  253.4 5.6 %collective-permute-start.17 = (bf16[248,128]{1,0:T(8,128)(2,1)S(1)}, bf16[248,128]{1,0:T(8,128)(2,1)S(1)}, u32[]{:S(2)}, u32[]{:S(2)}) collective-permute-start(bf16[248,128]{1,0:T(8,128)(2,1)S(1)} %get-tuple-element.123), channel_id=1, source_target_pairs={{0,16},{1,17},{2,18},{3,19},{4,20},{5,21},{6,22},{7,23},{8,24},{9,... | collective-permute-start | bytes 190472 | tf_op jit(solution)/shard_map/ppermute | solution.py:533
  255.2 6.1 %collective-permute-start.18 = (bf16[248,128]{1,0:T(8,128)(2,1)S(1)}, bf16[248,128]{1,0:T(8,128)(2,1)S(1)}, u32[]{:S(2)}, u32[]{:S(2)}) collective-permute-start(bf16[248,128]{1,0:T(8,128)(2,1)S(1)} %get-tuple-element.122), channel_id=1, source_target_pairs={{0,24},{1,25},{2,26},{3,27},{4,28},{5,29},{6,30},{7,31},{8,16},{9,... | collective-permute-start | bytes 190472 | tf_op jit(solution)/shard_map/ppermute | solution.py:533
  256.1 12.1 %collective-permute-start.23 = (f32[16,20,128]{2,0,1:T(8,128)S(1)}, f32[16,20,128]{2,0,1:T(8,128)S(1)}, u32[]{:S(2)}, u32[]{:S(2)}) collective-permute-start(f32[16,20,128]{2,0,1:T(8,128)S(1)} %bitcast.216), channel_id=1, source_target_pairs={{0,1},{1,0},{2,3},{3,2},{4,5},{5,4},{6,7},{7,6},{8,9},{9,8},{10,11... | collective-permute-start | bytes 491528 | tf_op jit(solution)/shard_map/ppermute | solution.py:533
  263.5 2.7 collective-permute-start.19
Sparse Core Ops, SparseCore 0:
  14.9 83.3 all-gather.2
  174.2 24.8 reduce-scatter.4
  233.9 25.0 reduce-scatter.6
where the time goes:
time: 282 us; the launch traced here: 277 us
  Pallas kernels  119 us (42%)
  waiting for transfers between devices  77 us (27%)
  local copies, waits for them, and re-layouts  24 us (9%)
  starting transfers between devices  23.1 us (8%)
  other arithmetic  18.8 us (7%)
  between operations  14.8 us (5%)
    pallas_call x1, Pallas kernels, run_middle(): pl.pallas_call(functools.partial(middle_kernel, pack, tiles), grid=(2 * p...  59.6 us
    ppermute x24, waiting for transfers between devices, swap(): return lax.ppermute(value, AX, [(i, i ^ mask) for i in range(self.n)])  44.5 us
    pallas_call x1, Pallas kernels, run_backward(): pl.pallas_call(functools.partial(backward_kernel, pack, heads, tiles), gr...  42.3 us
    all_gather x1, waiting for transfers between devices, on_device(): lax.all_gather(mover.tiled([narrow[:, :split], w_output, w_down]), AX, ax...  32.3 us
    ppermute x24, starting transfers between devices, swap(): return lax.ppermute(value, AX, [(i, i ^ mask) for i in range(self.n)])  23 us
    pallas_call x1, Pallas kernels, run_forward(): pl.pallas_call(functools.partial(forward_kernel, pack, heads), grid_spec=...  16.9 us
    unnamed x65, local copies, waits for them, and re-layouts  10.6 us
  transfers between devices with their start and end apart: 27, of which 14 were waited for; matrix products, arithmetic and copies ran while one was open for 9% of the time, Pallas kernels for 21%

commit v1 on v0

--- a/solution.py
+++ b/solution.py
@@ -79,14 +79,15 @@
         for _, cols in narrow:
             self.narrow_at.append(at)
             at += cols // (2 * LANES) * self.pair
+        self.wide_rows = at
         self.tall_at = []
         for rows, cols in tall:
             self.tall_at.append(at)
             at += cols // LANES * (rows // (2 * chips))
         self.used = at
 
-    def unpack(self, step, slabs, narrow_refs, tall_refs):
-        slabs = [[value[: self.used].astype(F32) for value in pair] for pair in slabs]
+    def unpack(self, step, slabs, narrow_refs, tall_slabs, tall_refs):
+        slabs = [[value[: self.wide_rows].astype(F32) for value in pair] for pair in slabs]
         at_row = pl.multiple_of(step * STEP_ROWS, 16)
         for (_, cols), start, out in zip(self.narrow, self.narrow_at, narrow_refs):
             tiles = cols // (2 * LANES)
@@ -101,9 +102,9 @@
             group = self.chips_per_step * 2 * own
             at_tall = pl.multiple_of(step * group, 16)
             for t in range(cols // LANES):
-                lo = start + t * own
+                lo = start - self.wide_rows + t * own
                 value = jnp.concatenate(
-                    [s[p][lo : lo + own] for s in slabs for p in range(2)], axis=0
+                    [s[p][lo : lo + own] for s in tall_slabs for p in range(2)], axis=0
                 )
                 out[pl.ds(at_tall, group), t * LANES : (t + 1) * LANES] = value.astype(BF)
 
@@ -135,6 +136,31 @@
             send_ref[j] = jnp.where(core == 0, second, first).astype(BF)
 
 
+def near_slabs(place_ref, mine_refs, other_refs):
+    first = place_ref[0] == 0
+    slabs = []
+    for mine_ref, other_ref in zip(mine_refs, other_refs):
+        mine, other = mine_ref[0].astype(F32), other_ref[0].astype(F32)
+        slabs.append([jnp.where(first, mine, other), jnp.where(first, other, mine)])
+    return slabs
+
+
+def near_specs(pack, rows):
+    def slab(j):
+        def index(s, lens_ref, starts_ref, place_ref):
+            far = (jnp.minimum(s, pack.steps - 1) * pack.chips_per_step + j) ^ place_ref[1]
+            turned = jnp.int32(0)
+            left = pack.chips
+            while left > 1:
+                turned = turned * 4 + far % 4
+                far, left = far // 4, left // 4
+            return turned, 0, 0
+
+        return pl.BlockSpec((1, rows, LANES), index)
+
+    return [slab(j) for j in range(pack.chips_per_step)]
+
+
 def forward_kernel(
     pack, heads,
     lens_ref, starts_ref, place_ref, *refs,
@@ -153,12 +179,8 @@
 
     @pl.when(step < pack.steps)
     def _():
-        first = place_ref[0] == 0
-        slabs = []
-        for mine_ref, other_ref in zip(mine_refs, other_refs):
-            mine, other = mine_ref[0].astype(F32), other_ref[0].astype(F32)
-            slabs.append([jnp.where(first, mine, other), jnp.where(first, other, mine)])
-        pack.unpack(step, slabs, [w_s.at[:, :wide], w_s.at[:, wide : wide + hd], w_s.at[:, wide + hd :]], [])
+        slabs = near_slabs(place_ref, mine_refs, other_refs)
+        pack.unpack(step, slabs, [w_s.at[:, :wide], w_s.at[:, wide : wide + hd], w_s.at[:, wide + hd :]], [], [])
         w_out[...] = w_s[pl.ds(pl.multiple_of(step * STEP_ROWS, 16), STEP_ROWS), :]
 
     tile = step - pack.steps
@@ -207,10 +229,15 @@
 
 def middle_kernel(
     pack, tiles,
-    lens_ref, starts_ref, core_ref, g_ref, x_ref, ob_ref, ct_ref, gpost_ref, gpre_ref, gffn_ref,
-    res_ref, dx1_ref, dob_ref, dgains_ref, keep_ref, send_ref,
-    wg_s, wu_s, wo_s, wd_s, ag_s, au_s, ao_s, ad_s, gain_s,
+    lens_ref, starts_ref, place_ref, *refs,
 ):
+    count = pack.chips_per_step
+    mine_refs, other_refs, refs = refs[:count], refs[count : 2 * count], refs[2 * count :]
+    (
+        g_ref, x_ref, ob_ref, ct_ref, gpost_ref, gpre_ref, gffn_ref,
+        res_ref, dx1_ref, dob_ref, dgains_ref, keep_ref, send_ref,
+        wg_s, wu_s, wo_s, wd_s, ag_s, au_s, ao_s, ad_s, gain_s,
+    ) = refs
     step = pl.program_id(0)
 
     @pl.when(step == 0)
@@ -221,7 +248,7 @@
     @pl.when(step < pack.steps)
     def _():
         slabs = [[g_ref[j, p] for p in range(2)] for j in range(pack.chips_per_step)]
-        pack.unpack(step, slabs, [wg_s, wu_s], [wo_s, wd_s])
+        pack.unpack(step, slabs, [wg_s, wu_s], near_slabs(place_ref, mine_refs, other_refs), [wo_s, wd_s])
 
     tile = step - pack.steps
 
@@ -268,7 +295,7 @@
 
     @pl.when(tile >= tiles)
     def _():
-        pack.pack(tile - tiles, core_ref[0], [ag_s, au_s], [ao_s, ad_s], keep_ref, send_ref)
+        pack.pack(tile - tiles, place_ref[0], [ag_s, au_s], [ao_s, ad_s], keep_ref, send_ref)
         dgains_ref[...] = gain_s[...]
 
 
@@ -379,24 +406,12 @@
     def fixed(width):
         return pl.BlockSpec((1, width), lambda s, *_: (0, 0))
 
-    def slab(j):
-        def index(s, lens_ref, starts_ref, place_ref):
-            far = (jnp.minimum(s, last) * count + j) ^ place_ref[1]
-            turned = jnp.int32(0)
-            left = pack.chips
-            while left > 1:
-                turned = turned * 4 + far % 4
-                far, left = far // 4, left // 4
-            return turned, 0, 0
-
-        return pl.BlockSpec((1, mine.shape[1], LANES), index)
-
     return pl.pallas_call(
         functools.partial(forward_kernel, pack, heads),
         grid_spec=pltpu.PrefetchScalarGridSpec(
             num_scalar_prefetch=3,
             grid=(pack.steps + slots // TILE,),
-            in_specs=[slab(j) for j in range(count)] * 2
+            in_specs=near_specs(pack, mine.shape[1]) * 2
             + [tile_spec(model), tile_spec(hd // 2), tile_spec(hd // 2), fixed(model), fixed(hd), fixed(hd)],
             out_specs=[
                 pl.BlockSpec((STEP_ROWS, cols), lambda s, *_: (jnp.minimum(s, last), 0)),
@@ -422,7 +437,7 @@
     )(lens, starts, place, *([mine] * count), *([other] * count), tokens, cos, sin, gin, gq, gk)
 
 
-def run_middle(pack, lens, starts, core, gathered, tokens, ob, cotangent, gpost, gpre, gffn):
+def run_middle(pack, lens, starts, place, mine, other, gathered, tokens, ob, cotangent, gpost, gpre, gffn):
     slots, model = tokens.shape
     wide = ob.shape[1]
     ff = pack.narrow[0][1]
@@ -430,37 +445,44 @@
     last = pack.steps - 1
 
     def tile_spec(width):
-        return pl.BlockSpec((TILE, width), lambda s: (jnp.clip(s - pack.steps, 0, tiles - 1), 0))
+        return pl.BlockSpec((TILE, width), lambda s, *_: (jnp.clip(s - pack.steps, 0, tiles - 1), 0))
+
+    def fixed(dims):
+        zeros = (0,) * len(dims)
+        return pl.BlockSpec(dims, lambda s, *_: zeros)
 
     def out_packed():
         return pl.BlockSpec(
             (pack.chips_per_step, pack.used, LANES),
-            lambda s: (jnp.maximum(s - pack.steps - tiles, 0), 0, 0),
+            lambda s, *_: (jnp.maximum(s - pack.steps - tiles, 0), 0, 0),
         )
 
     packed = pl.BlockSpec(
-        (pack.chips_per_step, 2, gathered.shape[2], LANES), lambda s: (jnp.minimum(s, last), 0, 0, 0)
+        (pack.chips_per_step, 2, gathered.shape[2], LANES), lambda s, *_: (jnp.minimum(s, last), 0, 0, 0)
     )
     return pl.pallas_call(
         functools.partial(middle_kernel, pack, tiles),
+        grid_spec=pltpu.PrefetchScalarGridSpec(
+        num_scalar_prefetch=3,
         grid=(2 * pack.steps + tiles,),
-        in_specs=[
-            smem(), smem(), smem(), packed, tile_spec(model), tile_spec(wide), tile_spec(model),
-            whole((1, model)), whole((1, model)), whole((1, model)),
+        in_specs=near_specs(pack, mine.shape[1]) * 2 + [
+            packed, tile_spec(model), tile_spec(wide), tile_spec(model),
+            fixed((1, model)), fixed((1, model)), fixed((1, model)),
         ],
         out_specs=[
-            tile_spec(model), tile_spec(model), tile_spec(wide), whole((3, 8, model)), out_packed(), out_packed(),
-        ],
-        out_shape=[
-            shape((slots, model), BF), shape((slots, model), F32), shape((slots, wide), BF),
-            shape((3, 8, model), F32),
-            shape((pack.chips, pack.used, LANES), BF), shape((pack.chips, pack.used, LANES), BF),
+            tile_spec(model), tile_spec(model), tile_spec(wide), fixed((3, 8, model)), out_packed(), out_packed(),
         ],
         scratch_shapes=[
             pltpu.VMEM((model, ff), BF), pltpu.VMEM((model, ff), BF), pltpu.VMEM((wide, model), BF),
             pltpu.VMEM((ff, model), BF),
             pltpu.VMEM((model, ff), F32), pltpu.VMEM((model, ff), F32), pltpu.VMEM((wide, model), F32),
             pltpu.VMEM((ff, model), F32), pltpu.VMEM((3, 8, model), F32),
+        ],
+        ),
+        out_shape=[
+            shape((slots, model), BF), shape((slots, model), F32), shape((slots, wide), BF),
+            shape((3, 8, model), F32),
+            shape((pack.chips, pack.used, LANES), BF), shape((pack.chips, pack.used, LANES), BF),
         ],
         compiler_params=params(60),
         cost_estimate=pl.CostEstimate(
@@ -468,7 +490,7 @@
             transcendentals=slots * ff,
         ),
         name="output_and_ffn",
-    )(lens, starts, core, gathered, tokens, ob, cotangent, gpost, gpre, gffn)
+    )(lens, starts, place, *([mine] * pack.chips_per_step), *([other] * pack.chips_per_step), gathered, tokens, ob, cotangent, gpost, gpre, gffn)
 
 
 def run_backward(pack, heads, lens, starts, core, weights, tokens, dx1, h1, qraw, kraw, qn, dob, kn, v, cos, sin, gin, gq, gk):
@@ -549,13 +571,8 @@
         tiles = [b.reshape(b.shape[0], -1, LANES).transpose(1, 0, 2).reshape(-1, LANES) for b in blocks]
         return jnp.concatenate(tiles, axis=0)
 
-    def gather_near(self, block):
-        got = block[None]
-        for digit in reversed(range(self.digits)):
-            got = jnp.concatenate(
-                [got] + [self.swap(got, j << (2 * digit + 1)) for j in (1, 2, 3)], axis=0
-            )
-        return got
+    def spread(self, got, digit):
+        return [got] + [self.swap(got, j << (2 * digit + 1)) for j in (1, 2, 3)]
 
     def by_digits(self, value):
         return value.reshape((4,) * self.digits + value.shape[1:])
@@ -648,9 +665,18 @@
     flat = jnp.pad(flat, (0, 8 * LANES - flat.shape[0])).reshape(8, LANES)
     narrow = mover.trade_halves([w_gate, w_up, w_query, w_key, w_value])
     split = w_gate.shape[1]
-    far = lax.all_gather(mover.tiled([narrow[:, :split], w_output, w_down]), AX, axis=0)
-    gathered = far.reshape(chips, 2, ffn.used, LANES)
-    mine = mover.gather_near(mover.tiled([narrow[:, split:], flat]))
+    far = lax.all_gather(mover.tiled([narrow[:, :split]]), AX, axis=0)
+    gathered = far.reshape(chips, 2, ffn.wide_rows, LANES)
+    down = list(reversed(range(mover.digits)))
+    mine = mover.tiled([narrow[:, split:], flat])[None]
+    tall = mover.tiled([w_output, w_down])[None]
+    mine = jnp.concatenate(mover.spread(mine, down[0]), axis=0)
+    for d in down[1:]:
+        tall, mine = lax.optimization_barrier((tall, mine))
+        tall = jnp.concatenate(mover.spread(tall, d + 1), axis=0)
+        mine = jnp.concatenate(mover.spread(mine, d), axis=0)
+    tall, mine = lax.optimization_barrier((tall, mine))
+    tall = mover.spread(tall, 0)
     other = mover.swap(mine)
     both = jnp.stack(mover.in_core_order(mine[:, attn.used], other[:, attn.used]), axis=1)
     order = [int("".join(reversed(format_base4(k, mover.digits))), 4) for k in range(chips)]
@@ -676,10 +702,13 @@
     weights, h1, qraw, kraw, qn, kn, v, ob = run_forward(
         attn, heads, seq_lens, seq_starts, place, mine, other, tokens, cos, sin, gin, gq, gk
     )
+    tall, ob = lax.optimization_barrier((tall, ob))
+    tall_mine = jnp.concatenate(tall, axis=0)
+    tall_other = mover.swap(tall_mine)
     result, dx1, dob, dgains, keep, send = run_middle(
-        ffn, seq_lens, seq_starts, core, gathered, tokens, ob, cotangent, gpost, gpre, gffn
-    )
-    up, down = list(range(mover.digits)), list(reversed(range(mover.digits)))
+        ffn, seq_lens, seq_starts, place, tall_mine, tall_other, gathered, tokens, ob, cotangent, gpost, gpre, gffn
+    )
+    up = list(range(mover.digits))
     cut = 3 * ffn.used // 32 * 8
     both = [mover.by_digits(keep), mover.by_digits(mover.swap(send))]
     near = mover.shares([v[..., :cut, :] for v in both], up[0], down)

time: 282 us -> 278 us (0.986)
  waiting for transfers between devices: 77 us -> 65.6 us
  starting transfers between devices: 23.1 us -> 28.3 us
    all_gather x1, waiting for transfers between devices: 32.3 us -> 5.43 us  [on_device(): far = lax.all_gather(mover.tiled([narrow[:, :split]]), AX, axis=0)]
    ppermute x24 -> x31, waiting for transfers between devices: 44.5 us -> 60.1 us  [swap(): return lax.ppermute(value, AX, [(i, i ^ mask) for i in range(self.n)])]
    ppermute x24 -> x31, starting transfers between devices: 23 us -> 28.1 us  [swap(): return lax.ppermute(value, AX, [(i, i ^ mask) for i in range(self.n)])]
    unnamed x65 -> x70, local copies, waits for them, and re-layouts: 10.6 us -> 11.1 us
  transfers between devices with their start and end apart: 27 -> 34, of which waited for: 14 -> 16; matrix products, arithmetic and copies ran while one was open for 9% -> 10% of each run, Pallas kernels for 21% -> 22%
where the time goes in v1:
time: 278 us; the launch traced here: 273 us
  Pallas kernels  120 us (43%)
  waiting for transfers between devices  65.6 us (24%)
  starting transfers between devices  28.3 us (10%)
  local copies, waits for them, and re-layouts  23.8 us (9%)
  other arithmetic  19.6 us (7%)
  between operations  14.8 us (5%)
    pallas_call x1, Pallas kernels, run_middle(): pl.pallas_call(functools.partial(middle_kernel, pack, tiles), grid_spec=p...  61.1 us
    ppermute x31, waiting for transfers between devices, swap(): return lax.ppermute(value, AX, [(i, i ^ mask) for i in range(self.n)])  60.1 us
    pallas_call x1, Pallas kernels, run_backward(): pl.pallas_call(functools.partial(backward_kernel, pack, heads, tiles), gr...  42.3 us
    ppermute x31, starting transfers between devices, swap(): return lax.ppermute(value, AX, [(i, i ^ mask) for i in range(self.n)])  28.1 us
    pallas_call x1, Pallas kernels, run_forward(): pl.pallas_call(functools.partial(forward_kernel, pack, heads), grid_spec=...  17 us
    unnamed x70, local copies, waits for them, and re-layouts  11.1 us
  transfers between devices with their start and end apart: 34, of which 16 were waited for; matrix products, arithmetic and copies ran while one was open for 10% of the time, Pallas kernels for 22%

profile of v1, /device:TPU:9, one launch (start us, length us, event | category | flops | bytes accessed | tf_op | source)
XLA Modules:
  0.0 272.8 jit_solution(4405267639004269829)
XLA Ops:
  7.3 0.8 slice_dynamic-update-slice_fusion.3
  8.2 0.8 slice_dynamic-update-slice_fusion.2
  9.0 0.8 constant_dynamic-update-slice_fusion.2
  9.8 0.7 constant_dynamic-update-slice_fusion.1
  10.5 0.7 constant_dynamic-update-slice_fusion
  11.2 0.7 collective-permute-start
  12.0 1.0 collective-permute-done
  13.0 0.7 copy_bitcast_fusion.1
  14.5 2.5 collective-permute-start.2
  17.5 2.3 collective-permute-done.2
  19.8 2.8 %collective-permute-done.3 = bf16[1,248,128]{2,1,0:T(8,128)(2,1)S(1)} collective-permute-done((bf16[1,248,128]{2,1,0:T(8,128)(2,1)S(1)}, bf16[1,248,128]{2,1,0:T(8,128)(2,1)S(1)}, u32[]{:S(2)}, u32[]{:S(2)}) %collective-permute-start.3) | collective-permute-done | bytes 63520 | tf_op jit(solution)/shard_map/ppermute | solution.py:555
  22.6 0.7 collective-permute-start.4
  23.3 1.2 collective-permute-start.7
  24.5 1.2 collective-permute-start.8
  26.0 1.6 collective-permute-start.5
  28.3 9.5 %collective-permute-done.5 = bf16[1,480,128]{2,1,0:T(8,128)(2,1)S(1)} collective-permute-done((bf16[1,480,128]{2,1,0:T(8,128)(2,1)S(1)}, bf16[1,480,128]{2,1,0:T(8,128)(2,1)S(1)}, u32[]{:S(2)}, u32[]{:S(2)}) %collective-permute-start.5) | collective-permute-done | bytes 122912 | tf_op jit(solution)/shard_map/ppermute | solution.py:555
  37.8 3.5 %collective-permute-done.6 = bf16[1,480,128]{2,1,0:T(8,128)(2,1)S(1)} collective-permute-done((bf16[1,480,128]{2,1,0:T(8,128)(2,1)S(1)}, bf16[1,480,128]{2,1,0:T(8,128)(2,1)S(1)}, u32[]{:S(2)}, u32[]{:S(2)}) %collective-permute-start.6) | collective-permute-done | bytes 122912 | tf_op jit(solution)/shard_map/ppermute | solution.py:555
  41.3 0.8 pad_maximum_fusion.2
  42.3 1.3 collective-permute-start.13
  43.8 1.9 multiply_sine_fusion
  45.7 1.3 collective-permute-start.10
  46.9 1.2 collective-permute-start.11
  49.0 17.0 %attention_forward.1 = (bf16[640,1536]{1,0:T(8,128)(2,1)}, bf16[1024,640]{1,0:T(8,128)(2,1)}, f32[1024,1024]{1,0:T(8,128)}, f32[1024,256]{1,0:T(8,128)S(1)}, bf1...) custom-call(s32[4]{0:T(128)S(1)} %copy-done.6, ...), custom_call_target="tpu_custom_call" | custom-call | flops 4160749568 | bytes 16777216 | tf_op jit(solution)/shard_map/attention_forward/pallas_call | solution.py:409
  66.2 12.0 %collective-permute-done.12 = bf16[4,480,128]{2,1,0:T(8,128)(2,1)} collective-permute-done((bf16[4,480,128]{2,1,0:T(8,128)(2,1)}, bf16[4,480,128]{2,1,0:T(8,128)(2,1)}, u32[]{:S(2)}, u32[]{:S(2)}) %collective-permute-start.12) | collective-permute-done | bytes 491552 | tf_op jit(solution)/shard_map/ppermute | solution.py:555
  78.2 1.1 constant_dynamic-update-slice_fusion.9
  79.3 1.1 constant_dynamic-update-slice_fusion.8
  80.4 1.1 constant_dynamic-update-slice_fusion.7
  81.5 1.1 constant_dynamic-update-slice_fusion.6.refs_0_.refs_1_
  82.6 0.7 collective-permute-start.14
  83.3 0.7 reshape.268.refs_8_
  84.0 0.7 reshape.269.refs_9_
  84.7 0.7 reshape.270.refs_10_
  85.4 1.7 collective-permute-done.14.refs_2_.refs_3_
  87.0 5.4 %all-gather.2.cloned.1.call-done = bf16[32,640,128]{2,1,0:T(8,128)(2,1)} async-done(((bf16[1,640,128]{2,1,0:T(8,128)(2,1)}), bf16[32,640,128]{2,1,0:T(8,128)(2,1)}) %all-gather.2.cloned.1.call-update) | async-done | bytes 5242896 | tf_op jit(solution)/shard_map/all_gather | solution.py:668
  92.5 61.1 %output_and_ffn.1 = (bf16[1024,640]{1,0:T(8,128)(2,1)}, f32[1024,640]{1,0:T(8,128)}, bf16[1024,1024]{1,0:T(8,128)(2,1)}, f32[3,8,640]{2,1,0:T(8,128)}, bf16[16,1...) custom-call(s32[4]{0:T(128)} %lens_ref.5, s32[4]{0:T(128)} %starts_ref.5, s32[2]{0:T(128)} %copy-done.7, ...), custom_call_target="tpu_custom_call" | custom-call | flops 28185722880 | bytes 37748736 | tf_op jit(solution)/shard_map/output_and_ffn/pallas_call | solution.py:463
  153.9 2.2 slice.159
  156.1 5.6 %collective-permute-done.15 = bf16[16,1120,128]{2,1,0:T(8,128)(2,1)} collective-permute-done((bf16[16,1120,128]{2,1,0:T(8,128)(2,1)}, bf16[16,1120,128]{2,1,0:T(8,128)(2,1)}, u32[]{:S(2)}, u32[]{:S(2)}) %collective-permute-start.15) | collective-permute-done | bytes 4587552 | tf_op jit(solution)/shard_map/ppermute | solution.py:555
  161.8 2.9 %add_convert_fusion = bf16[4,4,280,128]{3,2,1,0:T(8,128)(2,1)} fusion(bf16[4,4,1120,128]{3,2,1,0:T(8,128)(2,1)} %bitcast.15, bf16[4,4,1120,128]{3,2,1,0:T(8,128)(2,1)} %bitcast.196), kind=kLoop, calls=%fused_computation | loop fusion | flops 2293760 | bytes 3440640 | tf_op jit(solution)/shard_map/convert_element_type | solution.py:715
  164.7 2.2 slice.160
  166.9 2.7 %fusion.2 = (bf16[4,840,128]{2,1,0:T(8,128)(2,1)}, bf16[4,840,128]{2,1,0:T(8,128)(2,1)}, bf16[4,840,128]{2,1,0:T(8,128)(2,1)}, f32[4,840,128]{2,1,0:T(8,128)}) fusion(bf16[4,4,840,128]{3,2,1,0:T(8,128)(2,1)S(1)} %slice.160, s32[]{:T(128)S(6)} %select_n.183, bf16[4,4,840,128]{3,2,1,0:T(8,128)(2,1)S(1)} %slice.159, s32[]{:T(128)S(6)} %select_n.182, ...), kind=kLoop, calls=%fused_computation.13 | loop fusion | flops 6451200 | bytes 11182096 | tf_op jit(solution)/shard_map/convert_element_type | solution.py:589
  170.1 1.1 collective-permute-start.16
  171.7 1.2 collective-permute-start.18
  172.8 42.3 %attention_backward.1 = (f32[1024,640]{1,0:T(8,128)}, f32[8,640]{1,0:T(8,128)}, f32[8,256]{1,0:T(8,128)}, f32[8,256]{1,0:T(8,128)}, bf16[16,240,128]{2,1,0:T(8,128)(2,1)}, /*index=5*/bf16[16,240,128]{2,1,0:T(8,128)(2,1)}) custom-call(s32[4]{0:T(128)} %lens_ref.5, s32[4]{0:T(128)} %starts_ref.5, s32[1]{0:T(128)} %bitcast.core_ref, ...), custom_call_target="tpu_custom_call" | custom-call | flops 9395240960 | bytes 25165824 | tf_op jit(solution)/shard_map/attention_backward/pallas_call | solution.py:511
  215.2 0.9 reduce_sum.64
  216.2 0.7 reduce_sum.65
  217.0 0.7 reduce_sum.66
  218.0 2.3 pad_maximum_fusion.1
  220.3 0.9 copy-done.13
  221.5 1.1 collective-permute-start.19
  222.5 3.0 %fusion.16 = (bf16[840,128]{1,0:T(8,128)(2,1)}, bf16[840,128]{1,0:T(8,128)(2,1)}, bf16[840,128]{1,0:T(8,128)(2,1)}, f32[840,128]{1,0:T(8,128)S(1)}) fusion(f32[4,840,128]{2,1,0:T(8,128)S(1)} %copy-done.11, s32[]{:T(128)S(6)} %select_n.190, bf16[4,840,128]{2,1,0:T(8,128)(2,1)} %collective-permute-done.18, bf16[4,840,128]{2,1,0:T(8,128)(2,1)} %copy-done.14, ...), kind=kLoop, calls=%fused_computation.44 | loop fusion | flops 2903040 | bytes 5376016 | tf_op jit(solution)/shard_map/add | solution.py:588
  225.6 1.1 fusion.5
  226.7 1.8 collective-permute-start.27
  228.5 0.8 collective-permute-start.28
  229.7 0.8 collective-permute-start.20
  230.9 6.8 %collective-permute-done.27 = bf16[840,128]{1,0:T(8,128)(2,1)S(1)} collective-permute-done((bf16[840,128]{1,0:T(8,128)(2,1)}, bf16[840,128]{1,0:T(8,128)(2,1)S(1)}, u32[]{:S(2)}, u32[]{:S(2)}) %collective-permute-start.27) | collective-permute-done | bytes 215072 | tf_op jit(solution)/shard_map/ppermute | solution.py:555
  238.1 5.3 %collective-permute-done.28 = bf16[840,128]{1,0:T(8,128)(2,1)S(1)} collective-permute-done((bf16[840,128]{1,0:T(8,128)(2,1)}, bf16[840,128]{1,0:T(8,128)(2,1)S(1)}, u32[]{:S(2)}, u32[]{:S(2)}) %collective-permute-start.28) | collective-permute-done | bytes 215072 | tf_op jit(solution)/shard_map/ppermute | solution.py:555
  243.4 5.8 %collective-permute-done.29 = bf16[840,128]{1,0:T(8,128)(2,1)S(1)} collective-permute-done((bf16[840,128]{1,0:T(8,128)(2,1)}, bf16[840,128]{1,0:T(8,128)(2,1)S(1)}, u32[]{:S(2)}, u32[]{:S(2)}) %collective-permute-start.29) | collective-permute-done | bytes 215072 | tf_op jit(solution)/shard_map/ppermute | solution.py:555
  249.7 2.2 collective-permute-start.24
  252.4 1.7 collective-permute-start.30
  254.9 2.9 %collective-permute-done.25 = bf16[248,128]{1,0:T(8,128)(2,1)S(1)} collective-permute-done((bf16[248,128]{1,0:T(8,128)(2,1)S(1)}, bf16[248,128]{1,0:T(8,128)(2,1)S(1)}, u32[]{:S(2)}, u32[]{:S(2)}) %collective-permute-start.25) | collective-permute-done | bytes 63520 | tf_op jit(solution)/shard_map/ppermute | solution.py:555
  257.8 0.9 convert_element_type.307
  259.5 1.7 collective-permute-start.26
  262.4 0.7 copy.213
  263.2 0.7 copy.212
  (169 shorter events, 12.4 us)
Async XLA Ops:
  7.2 6.6 %copy-start.16 = (bf16[64,640]{1,0:T(8,128)(2,1)S(1)}, bf16[64,640]{1,0:T(8,128)(2,1)}, u32[]{:S(2)}) copy-start(bf16[64,640]{1,0:T(8,128)(2,1)} %param.33) | copy-start | bytes 245764
  7.2 6.8 %copy-start.18 = (bf16[32,640]{1,0:T(8,128)(2,1)S(1)}, bf16[32,640]{1,0:T(8,128)(2,1)}, u32[]{:S(2)}) copy-start(bf16[32,640]{1,0:T(8,128)(2,1)} %param.28) | copy-start | bytes 122884
  7.2 6.8 %copy-start.19 = (bf16[20]{0:T(256)(128)(2,1)S(1)}, bf16[20]{0:T(256)(128)(2,1)}, u32[]{:S(2)}) copy-start(bf16[20]{0:T(256)(128)(2,1)} %param.22) | copy-start | bytes 124
  7.2 6.8 %copy-start.20 = (bf16[8]{0:T(256)(128)(2,1)S(1)}, bf16[8]{0:T(256)(128)(2,1)}, u32[]{:S(2)}) copy-start(bf16[8]{0:T(256)(128)(2,1)} %param.26) | copy-start | bytes 52
  7.2 6.8 %copy-start.21 = (bf16[8]{0:T(256)(128)(2,1)S(1)}, bf16[8]{0:T(256)(128)(2,1)}, u32[]{:S(2)}) copy-start(bf16[8]{0:T(256)(128)(2,1)} %param.27) | copy-start | bytes 52
  7.2 6.8 %copy-start.22 = (bf16[20]{0:T(256)(128)(2,1)S(1)}, bf16[20]{0:T(256)(128)(2,1)}, u32[]{:S(2)}) copy-start(bf16[20]{0:T(256)(128)(2,1)} %param.29) | copy-start | bytes 124
  7.2 6.8 %copy-start.23 = (bf16[20]{0:T(256)(128)(2,1)S(1)}, bf16[20]{0:T(256)(128)(2,1)}, u32[]{:S(2)}) copy-start(bf16[20]{0:T(256)(128)(2,1)} %param.30) | copy-start | bytes 124
  7.3 6.8 %copy-start.24 = (bf16[20]{0:T(256)(128)(2,1)S(1)}, bf16[20]{0:T(256)(128)(2,1)}, u32[]{:S(2)}) copy-start(bf16[20]{0:T(256)(128)(2,1)} %param.34) | copy-start | bytes 124
  7.3 85.2 %all-gather.2.cloned.1.call-start = ((), (), s32[]{:S(2)}) async-start(), calls=%async_computation.2 | async-start | bytes 5406720 | tf_op jit(solution)/shard_map/all_gather | solution.py:668
  9.8 18.5 %copy-start.5 = (s32[4]{0:T(128)S(1)}, s32[4]{0:T(128)}, u32[]{:S(2)}) copy-start(s32[4]{0:T(128)} %starts_ref.5) | copy-start | bytes 52
  9.8 18.5 %copy-start.6 = (s32[4]{0:T(128)S(1)}, s32[4]{0:T(128)}, u32[]{:S(2)}) copy-start(s32[4]{0:T(128)} %lens_ref.5) | copy-start | bytes 52
  11.2 1.7 collective-permute-start
  13.7 206.5 %reduce-scatter.5.cloned.1.call-start = ((), (), s32[]{:S(2)}) async-start(), calls=%async_computation.3 | async-start | bytes 1433600 | tf_op jit(solution)/shard_map/reduce_scatter | solution.py:596
  14.4 29.4 %copy-start.25 = (s32[16]{0:T(128)S(1)}, s32[16]{0:T(128)}, u32[]{:S(2)}) copy-start(s32[16]{0:T(128)} %constant.189.clone) | copy-start | bytes 196
  14.4 3.2 %collective-permute-start.1 = (bf16[1,248,128]{2,1,0:T(8,128)(2,1)S(1)}, bf16[1,248,128]{2,1,0:T(8,128)(2,1)S(1)}, u32[]{:S(2)}, u32[]{:S(2)}) collective-permute-start(bf16[1,248,128]{2,1,0:T(8,128)(2,1)S(1)} %maximum_bitcast_fusion.4), channel_id=1, source_target_pairs={{0,8},{1,9},{2,10},{3,11},{4,12},{5,13},{6,14},{7,15},{8,0},{9,1},... | collective-permute-start | bytes 190472 | tf_op jit(solution)/shard_map/ppermute | solution.py:555
  14.5 5.3 %collective-permute-start.2 = (bf16[1,248,128]{2,1,0:T(8,128)(2,1)S(1)}, bf16[1,248,128]{2,1,0:T(8,128)(2,1)S(1)}, u32[]{:S(2)}, u32[]{:S(2)}) collective-permute-start(bf16[1,248,128]{2,1,0:T(8,128)(2,1)S(1)} %maximum_bitcast_fusion.4), channel_id=1, source_target_pairs={{0,16},{1,17},{2,18},{3,19},{4,20},{5,21},{6,22},{7,23},{8,24},{9,... | collective-permute-start | bytes 190472 | tf_op jit(solution)/shard_map/ppermute | solution.py:555
  16.9 5.7 %collective-permute-start.3 = (bf16[1,248,128]{2,1,0:T(8,128)(2,1)S(1)}, bf16[1,248,128]{2,1,0:T(8,128)(2,1)S(1)}, u32[]{:S(2)}, u32[]{:S(2)}) collective-permute-start(bf16[1,248,128]{2,1,0:T(8,128)(2,1)S(1)} %maximum_bitcast_fusion.4), channel_id=1, source_target_pairs={{0,24},{1,25},{2,26},{3,27},{4,28},{5,29},{6,30},{7,31},{8,16},{9,... | collective-permute-start | bytes 190472 | tf_op jit(solution)/shard_map/ppermute | solution.py:555
  22.6 5.3 %collective-permute-start.4 = (bf16[1,480,128]{2,1,0:T(8,128)(2,1)S(1)}, bf16[1,480,128]{2,1,0:T(8,128)(2,1)S(1)}, u32[]{:S(2)}, u32[]{:S(2)}) collective-permute-start(bf16[1,480,128]{2,1,0:T(8,128)(2,1)S(1)} %maximum_bitcast_fusion.2), channel_id=1, source_target_pairs={{0,8},{1,9},{2,10},{3,11},{4,12},{5,13},{6,14},{7,15},{8,0},{9,1},... | collective-permute-start | bytes 368648 | tf_op jit(solution)/shard_map/ppermute | solution.py:555
  23.3 18.8 %collective-permute-start.7 = (bf16[4,248,128]{2,1,0:T(8,128)(2,1)S(1)}, bf16[4,248,128]{2,1,0:T(8,128)(2,1)S(1)}, u32[]{:S(2)}, u32[]{:S(2)}) collective-permute-start(bf16[4,248,128]{2,1,0:T(8,128)(2,1)S(1)} %pad_maximum_fusion.3), channel_id=1, source_target_pairs={{0,2},{1,3},{2,0},{3,1},{4,6},{5,7},{6,4},{7,5},{8,10},{9,11},{10,... | collective-permute-start | bytes 761864 | tf_op jit(solution)/shard_map/ppermute | solution.py:555
  24.5 17.6 %collective-permute-start.8 = (bf16[4,248,128]{2,1,0:T(8,128)(2,1)S(1)}, bf16[4,248,128]{2,1,0:T(8,128)(2,1)S(1)}, u32[]{:S(2)}, u32[]{:S(2)}) collective-permute-start(bf16[4,248,128]{2,1,0:T(8,128)(2,1)S(1)} %pad_maximum_fusion.3), channel_id=1, source_target_pairs={{0,4},{1,5},{2,6},{3,7},{4,0},{5,1},{6,2},{7,3},{8,12},{9,13},{10,... | collective-permute-start | bytes 761864 | tf_op jit(solution)/shard_map/ppermute | solution.py:555
  25.8 16.4 %collective-permute-start.9 = (bf16[4,248,128]{2,1,0:T(8,128)(2,1)S(1)}, bf16[4,248,128]{2,1,0:T(8,128)(2,1)S(1)}, u32[]{:S(2)}, u32[]{:S(2)}) collective-permute-start(bf16[4,248,128]{2,1,0:T(8,128)(2,1)S(1)} %pad_maximum_fusion.3), channel_id=1, source_target_pairs={{0,6},{1,7},{2,4},{3,5},{4,2},{5,3},{6,0},{7,1},{8,14},{9,15},{10,... | collective-permute-start | bytes 761864 | tf_op jit(solution)/shard_map/ppermute | solution.py:555
  26.0 11.8 %collective-permute-start.5 = (bf16[1,480,128]{2,1,0:T(8,128)(2,1)S(1)}, bf16[1,480,128]{2,1,0:T(8,128)(2,1)S(1)}, u32[]{:S(2)}, u32[]{:S(2)}) collective-permute-start(bf16[1,480,128]{2,1,0:T(8,128)(2,1)S(1)} %maximum_bitcast_fusion.2), channel_id=1, source_target_pairs={{0,16},{1,17},{2,18},{3,19},{4,20},{5,21},{6,22},{7,23},{8,24},{9,... | collective-permute-start | bytes 368648 | tf_op jit(solution)/shard_map/ppermute | solution.py:555
  28.0 13.3 %collective-permute-start.6 = (bf16[1,480,128]{2,1,0:T(8,128)(2,1)S(1)}, bf16[1,480,128]{2,1,0:T(8,128)(2,1)S(1)}, u32[]{:S(2)}, u32[]{:S(2)}) collective-permute-start(bf16[1,480,128]{2,1,0:T(8,128)(2,1)S(1)} %maximum_bitcast_fusion.2), channel_id=1, source_target_pairs={{0,24},{1,25},{2,26},{3,27},{4,28},{5,29},{6,30},{7,31},{8,16},{9,... | collective-permute-start | bytes 368648 | tf_op jit(solution)/shard_map/ppermute | solution.py:555
  42.3 6.1 %collective-permute-start.13 = (bf16[16,248,128]{2,1,0:T(8,128)(2,1)S(1)}, bf16[16,248,128]{2,1,0:T(8,128)(2,1)S(1)}, u32[]{:S(2)}, u32[]{:S(2)}) collective-permute-start(bf16[16,248,128]{2,1,0:T(8,128)(2,1)S(1)} %pad_maximum_fusion.refs_0_.refs_1_), channel_id=1, source_target_pairs={{0,1},{1,0},{2,3},{3,2},{4,5},{5,4},{6,7},{7,6},{8,9},{9,8},{10,11... | collective-permute-start | bytes 3047432 | tf_op jit(solution)/shard_map/ppermute | solution.py:555
  43.6 22.4 %copy-start.7 = (s32[2]{0:T(128)}, s32[2]{0:T(128)S(1)}, u32[]{:S(2)}) copy-start(s32[2]{0:T(128)S(1)} %pad_add_fusion.place_ref) | copy-start | bytes 28
  45.6 20.4 %copy-start = (f32[1024,128]{1,0:T(8,128)}, f32[1024,128]{1,0:T(8,128)S(1)}, u32[]{:S(2)}) copy-start(f32[1024,128]{1,0:T(8,128)S(1)} %get-tuple-element.178.refs_6_.sin_ref) | copy-start | bytes 1572868
  45.7 20.4 %copy-start.1 = (f32[1024,128]{1,0:T(8,128)}, f32[1024,128]{1,0:T(8,128)S(1)}, u32[]{:S(2)}) copy-start(f32[1024,128]{1,0:T(8,128)S(1)} %get-tuple-element.179.refs_5_.cos_ref) | copy-start | bytes 1572868
  45.7 20.5 %collective-permute-start.10 = (bf16[4,480,128]{2,1,0:T(8,128)(2,1)}, bf16[4,480,128]{2,1,0:T(8,128)(2,1)}, u32[]{:S(2)}, u32[]{:S(2)}) collective-permute-start(bf16[4,480,128]{2,1,0:T(8,128)(2,1)} %pad_maximum_fusion.2), channel_id=1, source_target_pairs={{0,2},{1,3},{2,0},{3,1},{4,6},{5,7},{6,4},{7,5},{8,10},{9,11},{10,... | collective-permute-start | bytes 1474568 | tf_op jit(solution)/shard_map/ppermute | solution.py:555
  46.9 19.2 %collective-permute-start.11 = (bf16[4,480,128]{2,1,0:T(8,128)(2,1)}, bf16[4,480,128]{2,1,0:T(8,128)(2,1)}, u32[]{:S(2)}, u32[]{:S(2)}) collective-permute-start(bf16[4,480,128]{2,1,0:T(8,128)(2,1)} %pad_maximum_fusion.2), channel_id=1, source_target_pairs={{0,4},{1,5},{2,6},{3,7},{4,0},{5,1},{6,2},{7,3},{8,12},{9,13},{10,... | collective-permute-start | bytes 1474568 | tf_op jit(solution)/shard_map/ppermute | solution.py:555
  48.1 30.1 %collective-permute-start.12 = (bf16[4,480,128]{2,1,0:T(8,128)(2,1)}, bf16[4,480,128]{2,1,0:T(8,128)(2,1)}, u32[]{:S(2)}, u32[]{:S(2)}) collective-permute-start(bf16[4,480,128]{2,1,0:T(8,128)(2,1)} %pad_maximum_fusion.2), channel_id=1, source_target_pairs={{0,6},{1,7},{2,4},{3,5},{4,2},{5,3},{6,0},{7,1},{8,14},{9,15},{10,... | collective-permute-start | bytes 1474568 | tf_op jit(solution)/shard_map/ppermute | solution.py:555
  48.8 17.2 %copy-start.2 = (f32[1,640]{1,0:T(1,128)}, f32[1,640]{1,0:T(1,128)S(1)}, u32[]{:S(2)}) copy-start(f32[1,640]{1,0:T(1,128)S(1)} %reshape.263.refs_7_.gin_ref) | copy-start | bytes 7684
  48.9 17.2 %copy-start.3 = (f32[1,256]{1,0:T(1,128)}, f32[1,256]{1,0:T(1,128)S(1)}, u32[]{:S(2)}) copy-start(f32[1,256]{1,0:T(1,128)S(1)} %reshape.264.refs_8_.gq_ref) | copy-start | bytes 3076
  49.0 17.1 %copy-start.4 = (f32[1,256]{1,0:T(1,128)}, f32[1,256]{1,0:T(1,128)S(1)}, u32[]{:S(2)}) copy-start(f32[1,256]{1,0:T(1,128)S(1)} %reshape.265.refs_9_.gk_ref) | copy-start | bytes 3076
  66.1 16.5 %copy-start.8 = (f32[1024,256]{1,0:T(8,128)}, f32[1024,256]{1,0:T(8,128)S(1)}, u32[]{:S(2)}) copy-start(f32[1024,256]{1,0:T(8,128)S(1)} %get-tuple-element.84.kraw_ref) | copy-start | bytes 3145732
  66.1 16.5 %copy-start.9 = (bf16[1024,256]{1,0:T(8,128)(2,1)}, bf16[1024,256]{1,0:T(8,128)(2,1)S(1)}, u32[]{:S(2)}) copy-start(bf16[1024,256]{1,0:T(8,128)(2,1)S(1)} %get-tuple-element.90.k_ref) | copy-start | bytes 1572868
  66.1 16.5 %copy-start.10 = (bf16[1024,256]{1,0:T(8,128)(2,1)}, bf16[1024,256]{1,0:T(8,128)(2,1)S(1)}, u32[]{:S(2)}) copy-start(bf16[1024,256]{1,0:T(8,128)(2,1)S(1)} %get-tuple-element.91.v_ref) | copy-start | bytes 1572868
  82.6 9.9 %copy-start.15 = (bf16[16,480,128]{2,1,0:T(8,128)(2,1)}, bf16[16,480,128]{2,1,0:T(8,128)(2,1)S(1)}, u32[]{:S(2)}) copy-start(bf16[16,480,128]{2,1,0:T(8,128)(2,1)S(1)} %constant_dynamic-update-slice_fusion.6.refs_0_.refs_1_) | copy-start | bytes 5898244
  82.6 4.4 %collective-permute-start.14 = (bf16[16,480,128]{2,1,0:T(8,128)(2,1)S(1)}, bf16[16,480,128]{2,1,0:T(8,128)(2,1)}, u32[]{:S(2)}, u32[]{:S(2)}) collective-permute-start(bf16[16,480,128]{2,1,0:T(8,128)(2,1)S(1)} %constant_dynamic-update-slice_fusion.6.refs_0_.refs_1_), channel_id=1, source_target_pairs={{0,1},{1,0},{2,3},{3,2},{4,5},{5,4},{6,7},{7,6},{8,9},{9,8},{10,11... | collective-permute-start | bytes 5898248 | tf_op jit(solution)/shard_map/ppermute | solution.py:555
  153.6 8.1 %collective-permute-start.15 = (bf16[16,1120,128]{2,1,0:T(8,128)(2,1)}, bf16[16,1120,128]{2,1,0:T(8,128)(2,1)}, u32[]{:S(2)}, u32[]{:S(2)}) collective-permute-start(bf16[16,1120,128]{2,1,0:T(8,128)(2,1)} %get-tuple-element.88), channel_id=1, source_target_pairs={{0,1},{1,0},{2,3},{3,2},{4,5},{5,4},{6,7},{7,6},{8,9},{9,8},{10,11... | collective-permute-start | bytes 13762568 | tf_op jit(solution)/shard_map/ppermute | solution.py:555
  166.9 2.8 %copy-start.17 = (f32[3,8,640]{2,1,0:T(8,128)S(1)}, f32[3,8,640]{2,1,0:T(8,128)}, u32[]{:S(2)}) copy-start(f32[3,8,640]{2,1,0:T(8,128)} %get-tuple-element.97) | copy-start | bytes 184324
  169.7 85.2 %reduce-scatter.7.cloned.1.call-start = ((), (), s32[]{:S(2)}) async-start(), calls=%async_computation.4 | async-start | bytes 358400
  170.1 50.1 %collective-permute-start.16 = (bf16[4,840,128]{2,1,0:T(8,128)(2,1)}, bf16[4,840,128]{2,1,0:T(8,128)(2,1)S(1)}, u32[]{:S(2)}, u32[]{:S(2)}) collective-permute-start(bf16[4,840,128]{2,1,0:T(8,128)(2,1)} %get-tuple-element.99), channel_id=1, source_target_pairs={{0,2},{1,3},{2,0},{3,1},{4,6},{5,7},{6,4},{7,5},{8,10},{9,11},{10,... | collective-permute-start | bytes 2580488 | tf_op jit(solution)/shard_map/ppermute | solution.py:555
  171.3 49.0 %collective-permute-start.17 = (bf16[4,840,128]{2,1,0:T(8,128)(2,1)}, bf16[4,840,128]{2,1,0:T(8,128)(2,1)S(1)}, u32[]{:S(2)}, u32[]{:S(2)}) collective-permute-start(bf16[4,840,128]{2,1,0:T(8,128)(2,1)} %get-tuple-element.100), channel_id=1, source_target_pairs={{0,4},{1,5},{2,6},{3,7},{4,0},{5,1},{6,2},{7,3},{8,12},{9,13},{10,... | collective-permute-start | bytes 2580488 | tf_op jit(solution)/shard_map/ppermute | solution.py:555
  171.7 48.6 %collective-permute-start.18 = (bf16[4,840,128]{2,1,0:T(8,128)(2,1)}, bf16[4,840,128]{2,1,0:T(8,128)(2,1)}, u32[]{:S(2)}, u32[]{:S(2)}) collective-permute-start(bf16[4,840,128]{2,1,0:T(8,128)(2,1)} %get-tuple-element.101), channel_id=1, source_target_pairs={{0,6},{1,7},{2,4},{3,5},{4,2},{5,3},{6,0},{7,1},{8,14},{9,15},{10,... | collective-permute-start | bytes 2580488 | tf_op jit(solution)/shard_map/ppermute | solution.py:555
  215.2 7.4 %copy-start.11 = (f32[4,840,128]{2,1,0:T(8,128)S(1)}, f32[4,840,128]{2,1,0:T(8,128)}, u32[]{:S(2)}) copy-start(f32[4,840,128]{2,1,0:T(8,128)} %get-tuple-element.106) | copy-start | bytes 5160964
  220.2 0.9 copy-start.13
  220.2 1.2 copy-start.14
  221.5 4.1 %collective-permute-start.19 = (bf16[16,248,128]{2,1,0:T(8,128)(2,1)}, bf16[16,248,128]{2,1,0:T(8,128)(2,1)S(1)}, u32[]{:S(2)}, u32[]{:S(2)}) collective-permute-start(bf16[16,248,128]{2,1,0:T(8,128)(2,1)} %pad_maximum_fusion.1), channel_id=1, source_target_pairs={{0,1},{1,0},{2,3},{3,2},{4,5},{5,4},{6,7},{7,6},{8,9},{9,8},{10,11... | collective-permute-start | bytes 3047432 | tf_op jit(solution)/shard_map/ppermute | solution.py:555
  222.5 3.1 %copy-start.12 = (bf16[16,240,128]{2,1,0:T(8,128)(2,1)S(1)}, bf16[16,240,128]{2,1,0:T(8,128)(2,1)}, u32[]{:S(2)}) copy-start(bf16[16,240,128]{2,1,0:T(8,128)(2,1)} %get-tuple-element.104) | copy-start | bytes 2949124
  226.7 11.1 %collective-permute-start.27 = (bf16[840,128]{1,0:T(8,128)(2,1)}, bf16[840,128]{1,0:T(8,128)(2,1)S(1)}, u32[]{:S(2)}, u32[]{:S(2)}) collective-permute-start(bf16[840,128]{1,0:T(8,128)(2,1)} %get-tuple-element.119), channel_id=1, source_target_pairs={{0,8},{1,9},{2,10},{3,11},{4,12},{5,13},{6,14},{7,15},{8,0},{9,1},... | collective-permute-start | bytes 645128 | tf_op jit(solution)/shard_map/ppermute | solution.py:555
  228.5 14.9 %collective-permute-start.28 = (bf16[840,128]{1,0:T(8,128)(2,1)}, bf16[840,128]{1,0:T(8,128)(2,1)S(1)}, u32[]{:S(2)}, u32[]{:S(2)}) collective-permute-start(bf16[840,128]{1,0:T(8,128)(2,1)} %get-tuple-element.120), channel_id=1, source_target_pairs={{0,16},{1,17},{2,18},{3,19},{4,20},{5,21},{6,22},{7,23},{8,24},{9,... | collective-permute-start | bytes 645128 | tf_op jit(solution)/shard_map/ppermute | solution.py:555
  229.2 20.0 %collective-permute-start.29 = (bf16[840,128]{1,0:T(8,128)(2,1)}, bf16[840,128]{1,0:T(8,128)(2,1)S(1)}, u32[]{:S(2)}, u32[]{:S(2)}) collective-permute-start(bf16[840,128]{1,0:T(8,128)(2,1)} %get-tuple-element.121), channel_id=1, source_target_pairs={{0,24},{1,25},{2,26},{3,27},{4,28},{5,29},{6,30},{7,31},{8,16},{9,... | collective-permute-start | bytes 645128 | tf_op jit(solution)/shard_map/ppermute | solution.py:555
  229.7 19.7 %collective-permute-start.20 = (bf16[4,248,128]{2,1,0:T(8,128)(2,1)}, bf16[4,248,128]{2,1,0:T(8,128)(2,1)S(1)}, u32[]{:S(2)}, u32[]{:S(2)}) collective-permute-start(bf16[4,248,128]{2,1,0:T(8,128)(2,1)} %get-tuple-element.111), channel_id=1, source_target_pairs={{0,2},{1,3},{2,0},{3,1},{4,6},{5,7},{6,4},{7,5},{8,10},{9,11},{10,... | collective-permute-start | bytes 761864 | tf_op jit(solution)/shard_map/ppermute | solution.py:555
  230.5 18.9 %collective-permute-start.21 = (bf16[4,248,128]{2,1,0:T(8,128)(2,1)}, bf16[4,248,128]{2,1,0:T(8,128)(2,1)S(1)}, u32[]{:S(2)}, u32[]{:S(2)}) collective-permute-start(bf16[4,248,128]{2,1,0:T(8,128)(2,1)} %get-tuple-element.112), channel_id=1, source_target_pairs={{0,4},{1,5},{2,6},{3,7},{4,0},{5,1},{6,2},{7,3},{8,12},{9,13},{10,... | collective-permute-start | bytes 761864 | tf_op jit(solution)/shard_map/ppermute | solution.py:555
  237.7 11.7 %collective-permute-start.22 = (bf16[4,248,128]{2,1,0:T(8,128)(2,1)S(1)}, bf16[4,248,128]{2,1,0:T(8,128)(2,1)S(1)}, u32[]{:S(2)}, u32[]{:S(2)}) collective-permute-start(bf16[4,248,128]{2,1,0:T(8,128)(2,1)S(1)} %get-tuple-element.113), channel_id=1, source_target_pairs={{0,6},{1,7},{2,4},{3,5},{4,2},{5,3},{6,0},{7,1},{8,14},{9,15},{10,... | collective-permute-start | bytes 761864 | tf_op jit(solution)/shard_map/ppermute | solution.py:555
  249.6 5.3 %collective-permute-start.23 = (bf16[248,128]{1,0:T(8,128)(2,1)S(1)}, bf16[248,128]{1,0:T(8,128)(2,1)S(1)}, u32[]{:S(2)}, u32[]{:S(2)}) collective-permute-start(bf16[248,128]{1,0:T(8,128)(2,1)S(1)} %get-tuple-element.142), channel_id=1, source_target_pairs={{0,8},{1,9},{2,10},{3,11},{4,12},{5,13},{6,14},{7,15},{8,0},{9,1},... | collective-permute-start | bytes 190472 | tf_op jit(solution)/shard_map/ppermute | solution.py:555
  249.7 5.2 %collective-permute-start.24 = (bf16[248,128]{1,0:T(8,128)(2,1)S(1)}, bf16[248,128]{1,0:T(8,128)(2,1)S(1)}, u32[]{:S(2)}, u32[]{:S(2)}) collective-permute-start(bf16[248,128]{1,0:T(8,128)(2,1)S(1)} %get-tuple-element.141), channel_id=1, source_target_pairs={{0,16},{1,17},{2,18},{3,19},{4,20},{5,21},{6,22},{7,23},{8,24},{9,... | collective-permute-start | bytes 190472 | tf_op jit(solution)/shard_map/ppermute | solution.py:555
  251.9 5.9 %collective-permute-start.25 = (bf16[248,128]{1,0:T(8,128)(2,1)S(1)}, bf16[248,128]{1,0:T(8,128)(2,1)S(1)}, u32[]{:S(2)}, u32[]{:S(2)}) collective-permute-start(bf16[248,128]{1,0:T(8,128)(2,1)S(1)} %get-tuple-element.140), channel_id=1, source_target_pairs={{0,24},{1,25},{2,26},{3,27},{4,28},{5,29},{6,30},{7,31},{8,16},{9,... | collective-permute-start | bytes 190472 | tf_op jit(solution)/shard_map/ppermute | solution.py:555
  252.4 10.0 %collective-permute-start.30 = (f32[16,20,128]{2,0,1:T(8,128)S(1)}, f32[16,20,128]{2,0,1:T(8,128)S(1)}, u32[]{:S(2)}, u32[]{:S(2)}) collective-permute-start(f32[16,20,128]{2,0,1:T(8,128)S(1)} %bitcast.215), channel_id=1, source_target_pairs={{0,1},{1,0},{2,3},{3,2},{4,5},{5,4},{6,7},{7,6},{8,9},{9,8},{10,11... | collective-permute-start | bytes 491528 | tf_op jit(solution)/shard_map/ppermute | solution.py:555
  259.5 4.5 %collective-permute-start.26 = (f32[6,20,128]{2,1,0:T(8,128)S(1)}, f32[6,20,128]{2,1,0:T(8,128)S(1)}, u32[]{:S(2)}, u32[]{:S(2)}) collective-permute-start(f32[6,20,128]{2,1,0:T(8,128)S(1)} %dynamic-slice_bitcast_fusion), channel_id=1, source_target_pairs={{0,1},{1,0},{2,3},{3,2},{4,5},{5,4},{6,7},{7,6},{8,9},{9,8},{10,11... | collective-permute-start | bytes 184328 | tf_op jit(solution)/shard_map/ppermute | solution.py:555
Sparse Core Ops, SparseCore 0:
  13.9 78.5 all-gather.1
  169.8 25.7 reduce-scatter.4
  229.8 24.9 reduce-scatter.6
